TPU v7x, 256 devices: a whole 4x4x8 slice. The times are simulated.
256 devices in a mesh: seq: 64 (over y, z, core), batch: 4 (over x).
Axes of the slice: x: 4, y: 4, z: 8, core: 2. Of those that a mesh axis runs over, the one named last changes fastest.
Arguments:
- token_ids: int32 [262144], P(('batch', 'seq')), parts along dimension 0, may hold values from 0 to 4
- embed_table: bfloat16 [5, 256], replicated, may hold values from -6 to 6
- input_weight_matrix: bfloat16 [256, 1064], replicated, may hold values from -0.375 to 0.375
- output_weight_matrix: bfloat16 [512, 256], replicated, may hold values from -0.25 to 0.25
- conv_weight: float32 [2, 4, 512], replicated, may hold values from -3 to 3
- dt_bias: float32 [2, 8], replicated, may hold values from -1 to 1
- decay_rate: float32 [2, 8], replicated, may hold values from 0 to 0.05
- skip_gain: float32 [2, 8], replicated, may hold values from -4 to 4
- norm_gain: float32 [2, 512], replicated, may hold values from 0.1 to 1.9
Outputs:
- hidden: bfloat16 [262144, 256], P(('batch', 'seq')), parts along dimension 0
There are 4 independent parts, one for each index of `batch`. A program takes and returns all parts, laid end to end along the dimension named above; an argument that names none is the same for every part. Nothing has to cross between parts.
All inputs are finite; a program needn't handle non-finite values.
Results may differ from a plain program's by a relative error of at most 0.0029.
The roundings to bfloat16 on the way count: a program that leaves them out, or rounds other values in their place, can miss the bound.
Values may be sent and summed in bfloat16 or wider, within the bound.
A program may use at most 128 MiB of HBM per device.

v0:
```python
import jax
import jax.numpy as jnp
from jax import lax
from jax.sharding import PartitionSpec as P

E = 512
NS = 16
P_SIZE = 64
KW = 4
BLK = 128
H = 8


EPSILON = 1e-05


def carried_in(value, axis, join, neutral, backward):
    count, mine = (lax.axis_size(axis), lax.axis_index(axis))
    pieces = jax.tree.map(lambda part: lax.all_gather(part, axis), value)
    if backward:
        pieces = jax.tree.map(lambda part: part[::-1], pieces)
        mine = count - 1 - mine
    running = jax.tree.map(
        lambda part, zero: jnp.full_like(part, 0) + jnp.asarray(zero, part.dtype), value, neutral
    )

    def hop(position, running):
        longer = join(running, jax.tree.map(lambda part: part[position], pieces))
        return jax.tree.map(lambda new, old: jnp.where(position < mine, new, old), longer, running)

    return lax.fori_loop(0, count - 1, hop, running)


def swapped(block, axis, bit):
    count = lax.axis_size(axis)
    route = []
    for low in range(count):
        high = low | 1 << bit
        if high != low and high < count:
            route += [(low, high), (high, low)]
    return lax.ppermute(block, axis, route)


def padded(cells, sides, width):
    for axis, dim in sides:
        count = lax.axis_size(axis)
        ends = count - 1
        head = lax.slice_in_dim(cells, 0, width, axis=dim)
        tail = lax.slice_in_dim(cells, cells.shape[dim] - width, cells.shape[dim], axis=dim)
        cells = jnp.concatenate(
            [
                lax.ppermute(tail, axis, [(i, (i + 1) % count) for i in range(ends)]),
                cells,
                lax.ppermute(head, axis, [((i + 1) % count, i) for i in range(ends)]),
            ],
            axis=dim,
        )
    return cells


def complement(ids):
    return jnp.where(ids < 4, 3 - ids, ids)


def embed_rows(ids, embed_table):
    onehot = (ids[:, None] == jnp.arange(5, dtype=jnp.int32)[None, :]).astype(jnp.bfloat16)
    return jnp.dot(onehot, embed_table, preferred_element_type=jnp.float32).astype(jnp.bfloat16)


def block_step(state, pieces):
    highest = lax.Precision.HIGHEST
    inner_x, log_decay, step, b_part, c_part = pieces
    count = log_decay.shape[0]
    cumul = jnp.cumsum(log_decay, axis=0)
    index = jnp.arange(count)
    lower = index[:, None] >= index[None, :]
    spread = cumul[:, None, :] - cumul[None, :, :]
    decay = jnp.exp(jnp.where(lower[:, :, None], spread, -1e30))
    scores = jnp.dot(c_part, b_part.T, precision=highest)
    weighted = inner_x * step[:, :, None]
    inner = jnp.einsum("trh,rhp->thp", scores[:, :, None] * decay, weighted, precision=highest)
    carried = jnp.exp(cumul)[:, :, None] * jnp.einsum(
        "tn,hpn->thp", c_part, state, precision=highest
    )
    tail = jnp.exp(cumul[-1][None, :] - cumul)
    new_state = jnp.exp(cumul[-1])[:, None, None] * state + jnp.einsum(
        "rh,rhp,rn->hpn", tail, weighted, b_part, precision=highest
    )
    return (new_state, inner + carried)


def join_carry(earlier, later):
    return (earlier[0] * later[0], earlier[1] * later[0][:, :, None, None] + later[1])


def processor_sequence(inner_x, log_decay, step, b_part, c_part, backward):
    if backward:
        inner_x = jnp.flip(inner_x, axis=1)
        log_decay = jnp.flip(log_decay, axis=1)
        step = jnp.flip(step, axis=1)
        b_part = jnp.flip(b_part, axis=1)
        c_part = jnp.flip(c_part, axis=1)
    strands = log_decay.shape[0]
    rows = log_decay.shape[1]
    blocks = rows // BLK

    def split(value):
        return jnp.swapaxes(value.reshape((strands, blocks, BLK) + value.shape[2:]), 0, 1)

    init = jnp.zeros((strands, H, P_SIZE, NS), jnp.float32)
    pieces = (split(inner_x), split(log_decay), split(step), split(b_part), split(c_part))
    end_state, outputs = lax.scan(jax.vmap(block_step), init, pieces)
    outputs = jnp.swapaxes(outputs, 0, 1).reshape(strands, rows, H, P_SIZE)
    total = jnp.exp(jnp.sum(log_decay, axis=1))
    identity = (jnp.ones_like(total), jnp.zeros_like(end_state))
    if backward:
        incoming = carried_in((total, end_state), "seq", join_carry, identity, True)[1]
    else:
        incoming = carried_in((total, end_state), "seq", join_carry, identity, False)[1]
    reach = jnp.exp(jnp.cumsum(log_decay, axis=1))
    outputs = outputs + reach[..., None] * jnp.einsum(
        "sln,shpn->slhp", c_part, incoming, precision=lax.Precision.HIGHEST
    )
    if backward:
        outputs = jnp.flip(outputs, axis=1)
    return outputs


def per_device(
    token_ids,
    embed_table,
    input_weight_matrix,
    output_weight_matrix,
    conv_weight,
    dt_bias,
    decay_rate,
    skip_gain,
    norm_gain,
):
    rows = token_ids.shape[0]
    paired_strand = token_ids
    for bit in range(lax.axis_size("seq").bit_length() - 1):
        paired_strand = swapped(paired_strand, "seq", bit)
    second_ids = complement(paired_strand[::-1])
    forward_direction_params = (0, 0)
    behind_params = (1, 1)
    feature_vectors = jnp.stack(
        [embed_rows(token_ids, embed_table), embed_rows(second_ids, embed_table)]
    )
    projected = jnp.einsum(
        "zmx,xf->zmf", feature_vectors, input_weight_matrix, preferred_element_type=jnp.float32
    ).astype(jnp.bfloat16)
    values = projected[:, :, E : 2 * E]
    rim = KW - 1
    edges = jnp.concatenate([values[:, :rim], values[:, rows - rim :]], axis=1)
    extended = padded(edges, (("seq", 1),), rim)
    padded_input = jnp.concatenate(
        [extended[:, :rim], values, extended[:, 3 * rim :]], axis=1
    ).astype(jnp.float32)
    gate = projected[:, :, :E].astype(jnp.float32)
    b_part = projected[:, :, 2 * E : 2 * E + NS].astype(jnp.float32)
    c_part = projected[:, :, 2 * E + NS : 2 * E + 2 * NS].astype(jnp.float32)
    raw = projected[:, :, 2 * E + 2 * NS :].astype(jnp.float32)
    mixer_output = None
    for backward, params in ((False, forward_direction_params), (True, behind_params)):
        taps = jnp.stack([conv_weight[k] for k in params])
        bias = jnp.stack([dt_bias[k] for k in params])
        rate = jnp.stack([decay_rate[k] for k in params])
        skip = jnp.stack([skip_gain[k] for k in params])
        gain = jnp.stack([norm_gain[k] for k in params])
        acc = None
        for j in range(KW):
            begin = 2 * (KW - 1) - j if backward else j
            term = taps[:, j][:, None, :] * padded_input[:, begin : begin + rows]
            acc = term if acc is None else acc + term
        inner_x = jax.nn.silu(acc).reshape(2, rows, H, P_SIZE)
        step = jax.nn.softplus(raw + bias[:, None, :])
        log_decay = -rate[:, None, :] * step
        outputs = (
            processor_sequence(inner_x, log_decay, step, b_part, c_part, backward)
            + skip[:, None, :, None] * inner_x
        )
        gated = outputs * jax.nn.silu(gate).reshape(2, rows, H, P_SIZE)
        meansq = jnp.mean(gated * gated, axis=-1, keepdims=True)
        normed = (gated * lax.rsqrt(meansq + EPSILON) * gain.reshape(2, 1, H, P_SIZE)).reshape(
            2, rows, E
        )
        mixer_output = normed if mixer_output is None else mixer_output + normed
    mixer_output = mixer_output.astype(jnp.bfloat16)
    strand_out = jnp.einsum(
        "qtf,fg->qtg", mixer_output, output_weight_matrix, preferred_element_type=jnp.float32
    ).astype(jnp.bfloat16)
    mirrored = strand_out[1]
    for bit in range(lax.axis_size("seq").bit_length() - 1):
        mirrored = swapped(mirrored, "seq", bit)
    other = mirrored[::-1, ::-1]
    hidden = (
        feature_vectors[0].astype(jnp.float32)
        + strand_out[0].astype(jnp.float32)
        + other.astype(jnp.float32)
    )
    return hidden.astype(jnp.bfloat16)


def solution(mesh):
    placed = (P(("batch", "seq")), P(), P(), P(), P(), P(), P(), P(), P())
    return jax.shard_map(
        per_device, mesh=mesh, in_specs=placed, out_specs=P(("batch", "seq"), None), check_vma=False
    )
```

profile of v0, /device:TPU:1, one launch (start us, length us, event | category | flops | bytes accessed | tf_op | source)
XLA Modules:
  0.0 741.5 jit_solution(15624175950881066309)
XLA Ops:
  20.5 5.2 collective-permute-start.3
  38.4 7.6 %collective-permute-start.6 = (bf16[2,3,512]{1,2,0:T(8,128)(2,1)}, bf16[2,3,512]{1,2,0:T(8,128)(2,1)S(1)}, u32[]{:S(2)}, u32[]{:S(2)}) collective-permute-start(bf16[2,3,512]{1,2,0:T(8,128)(2,1)} %get-tuple-element.450), channel_id=1, source_target_pairs={{0,4},{4,8},{8,12},{12,16},{16,20},{20,24},{24,28},{28,32},{32,36}... | collective-permute-start | bytes 18440 | tf_op jit(solution)/shard_map/ppermute | solution.py:52
  51.7 4.5 reduce-window.16
  56.9 4.5 reduce-window.14
  66.4 46.8 %all-gather.5 = f32[64,2,8]{2,1,0:T(2,128)S(1)} all-gather(f32[1,2,8]{2,1,0:T(2,128)S(1)} %exponential_bitcast_fusion), channel_id=4, replica_groups=mesh['seq'=64,'batch'=4] {'seq'}, dimensions={0}, use_global_device_ids=true | all-gather | bytes 4160 | tf_op jit(solution)/shard_map/all_gather | solution.py:19
  117.2 45.7 %all-gather.4 = f32[64,2,8]{2,1,0:T(2,128)} all-gather(f32[1,2,8]{2,1,0:T(2,128)S(1)} %exponential_bitcast_fusion.1), channel_id=2, replica_groups=mesh['seq'=64,'batch'=4] {'seq'}, dimensions={0}, use_global_device_ids=true | all-gather | bytes 4160 | tf_op jit(solution)/shard_map/all_gather | solution.py:19
  168.9 9.9 %divide_multiply_fusion.1 = (f32[2,1024,512]{1,2,0:T(8,128)}, f32[2,1024,512]{1,2,0:T(8,128)}) fusion(f32[2,1030,512]{1,2,0:T(8,128)S(1)} %convert_element_type.55, f32[2,512]{1,0:T(2,128)S(1)} %bitcast.314, f32[2,512]{1,0:T(2,128)S(1)} %bitcast.315, f32[2,512]{1,0:T(2,128)S(1)} %bitcast.316, f32[2,512]{1,0:T(2,128)S(1)} %bitcast.317, ...), kind=kLoop, calls=%fused_computation.115 | loop fusion | flops 23068672 | bytes 37781504 | tf_op jit(solution)/shard_map/jit(silu)/mul | solution.py:176
  178.8 7.3 rev.35
  186.1 4.7 bitcast_bitcast_fusion
  193.3 93.8 %while.56 = (s32[]{:T(128)}, f32[2,8,64,16]{2,3,1,0:T(8,128)S(1)}, f32[8,2,128,8,64]{2,4,3,1,0:T(8,128)}, f32[8,2,128,8]{3,2,1,0:T(8,128)}, f32[8,2,128,8,64]{2,...) while((s32[]{:T(128)}, f32[2,8,64,16]{2,3,1,0:T(8,128)S(1)}, ...), condition=%wide.region_11.12_spmd.clone, body=%wide.region_9.11_spmd.clone.sunk | while | flops 259637248 | bytes 3386888 | solution.py:112
  296.5 93.9 %while.54 = (s32[]{:T(128)}, f32[2,8,64,16]{2,3,1,0:T(8,128)S(1)}, f32[8,2,128,8,64]{2,4,3,1,0:T(8,128)}, f32[8,2,128,8]{3,2,1,0:T(8,128)}, f32[8,2,128,8,64]{2,...) while((s32[]{:T(128)}, f32[2,8,64,16]{2,3,1,0:T(8,128)S(1)}, ...), condition=%wide.region_2.3_spmd.clone, body=%wide.region_0.2_spmd.clone.sunk | while | flops 259637248 | bytes 3386888 | solution.py:112
  324.8 4.1 fusion.160
  348.3 4.1 fusion.160
  391.1 7.8 %rev.40 = f32[64,2,8,64,16]{3,4,2,1,0:T(8,128)} reverse(f32[64,2,8,64,16]{3,4,2,1,0:T(8,128)} %bitcast.293), dimensions={0} | reverse | bytes 8388608 | tf_op jit(solution)/shard_map/rev | solution.py:21
  398.9 105.7 %while.57 = (s32[]{:T(128)}, f32[2,8,64,16]{2,3,1,0:T(8,128)S(1)}, s32[]{:T(128)}, f32[64,2,8]{2,1,0:T(2,128)}, f32[64,2,8,64,16]{3,4,2,1,0:T(8,128)}, /*index=5*/s32[]{:T(128)}, s32[]{:T(128)}) while((s32[]{:T(128)}, f32[2,8,64,16]{2,3,1,0:T(8,128)S(1)}, s32[]{:T(128)}, f32[64,2,8]{2,1,0:T(2,128)}, ...), condition=%wide.region_16.17_spmd.clone, body=%wide.region_15.16_spmd.clone.sunk | while | flops 65540 | bytes 196905 | solution.py:31
  504.6 6.7 bitcast_add_fusion.2
  511.4 7.3 rev.41
  518.7 105.7 %while.55 = (s32[]{:T(128)}, f32[2,8,64,16]{2,3,1,0:T(8,128)S(1)}, s32[]{:T(128)}, f32[64,2,8]{2,1,0:T(2,128)}, f32[64,2,8,64,16]{3,4,2,1,0:T(8,128)}, /*index=5*/s32[]{:T(128)}, s32[]{:T(128)}) while((s32[]{:T(128)}, f32[2,8,64,16]{2,3,1,0:T(8,128)S(1)}, s32[]{:T(128)}, f32[64,2,8]{2,1,0:T(2,128)}, ...), condition=%wide.region_7.8_spmd.clone, body=%wide.region_6.7_spmd.clone.sunk | while | flops 65540 | bytes 196905 | solution.py:31
  624.4 9.0 %multiply_reduce_fusion.1 = (f32[2,1024,8]{1,2,0:T(8,128)S(1)}, f32[2,1024,8,64]{1,3,2,0:T(8,128)S(1)}, f32[2,1024,8]{1,2,0:T(8,128)S(1)}, f32[2,1024,8,64]{1,3,2,0:T(8,128)S(1)}) fusion(f32[2,8]{1,0:T(2,128)S(1)} %get-tuple-element.475, f32[2,1024,8]{1,2,0:T(8,128)S(1)} %bitcast.306, f32[2,1024,8,64]{1,3,2,0:T(8,128)} %rev.41, ...), kind=kOutput, calls=%fused_computation.114 | convolution fusion | flops 219119616 | bytes 27590784 | tf_op jit(solution)/shard_map/sln,shpn->slhp/dot_general | solution.py:121
  638.2 13.0 %collective-permute-done.9 = bf16[1024,256]{1,0:T(8,128)(2,1)S(1)} collective-permute-done((bf16[1024,256]{1,0:T(8,128)(2,1)S(1)}, bf16[1024,256]{1,0:T(8,128)(2,1)S(1)}, u32[]{:S(2)}, u32[]{:S(2)}) %collective-permute-start.9) | collective-permute-done | bytes 524320 | tf_op jit(solution)/shard_map/ppermute | solution.py:41
  652.7 24.4 %collective-permute-done.10 = bf16[1024,256]{1,0:T(8,128)(2,1)S(1)} collective-permute-done((bf16[1024,256]{1,0:T(8,128)(2,1)S(1)}, bf16[1024,256]{1,0:T(8,128)(2,1)S(1)}, u32[]{:S(2)}, u32[]{:S(2)}) %collective-permute-start.10) | collective-permute-done | bytes 524320 | tf_op jit(solution)/shard_map/ppermute | solution.py:41
  679.7 25.9 %collective-permute-done.11 = bf16[1024,256]{1,0:T(8,128)(2,1)S(1)} collective-permute-done((bf16[1024,256]{1,0:T(8,128)(2,1)S(1)}, bf16[1024,256]{1,0:T(8,128)(2,1)S(1)}, u32[]{:S(2)}, u32[]{:S(2)}) %collective-permute-start.11) | collective-permute-done | bytes 524320 | tf_op jit(solution)/shard_map/ppermute | solution.py:41
  705.6 13.0 %collective-permute-done.12 = bf16[1024,256]{1,0:T(8,128)(2,1)S(1)} collective-permute-done((bf16[1024,256]{1,0:T(8,128)(2,1)S(1)}, bf16[1024,256]{1,0:T(8,128)(2,1)S(1)}, u32[]{:S(2)}, u32[]{:S(2)}) %collective-permute-start.12) | collective-permute-done | bytes 524320 | tf_op jit(solution)/shard_map/ppermute | solution.py:41
  718.6 13.3 %collective-permute-done.13 = bf16[1024,256]{1,0:T(8,128)(2,1)S(1)} collective-permute-done((bf16[1024,256]{1,0:T(8,128)(2,1)S(1)}, bf16[1024,256]{1,0:T(8,128)(2,1)S(1)}, u32[]{:S(2)}, u32[]{:S(2)}) %collective-permute-start.13) | collective-permute-done | bytes 524320 | tf_op jit(solution)/shard_map/ppermute | solution.py:41
  (612 shorter events, 459.4 us)
Async XLA Ops:
  6.5 28.2 %copy-start = (bf16[256,1064]{0,1:T(8,128)(2,1)S(1)}, bf16[256,1064]{0,1:T(8,128)(2,1)}, u32[]{:S(2)}) copy-start(bf16[256,1064]{0,1:T(8,128)(2,1)} %param.19) | copy-start | bytes 1634308
  6.5 384.5 %all-gather.11.cloned.1.call-start = ((), (), s32[]{:S(2)}) async-start(), calls=%async_computation.1 | async-start | bytes 8519680 | tf_op jit(solution)/shard_map/all_gather | solution.py:19
  6.5 8.1 %collective-permute-start = (s32[1024]{0:T(1024)}, s32[1024]{0:T(1024)S(1)}, u32[]{:S(2)}, u32[]{:S(2)}) collective-permute-start(s32[1024]{0:T(1024)} %param.17), channel_id=1, source_target_pairs={{0,4},{4,0},{8,12},{12,8},{16,20},{20,16},{24,28},{28,24},{32,36},... | collective-permute-start | bytes 12296 | tf_op jit(solution)/shard_map/ppermute | solution.py:41
  10.8 27.5 %copy-start.6 = (bf16[1024,256]{1,0:T(8,128)(2,1)}, bf16[1024,256]{1,0:T(8,128)(2,1)S(1)}, u32[]{:S(2)}) copy-start(bf16[1024,256]{1,0:T(8,128)(2,1)S(1)} %convolution_convert_fusion.3) | copy-start | bytes 1572868
  14.7 2.5 collective-permute-start.1
  17.1 3.4 collective-permute-start.2
  20.5 6.4 collective-permute-start.3
  26.9 2.8 collective-permute-start.4
  29.6 4.0 collective-permute-start.5
  36.1 11.8 %copy-start.4 = (bf16[2,1024,1064]{1,2,0:T(8,128)(2,1)}, bf16[2,1024,1064]{1,2,0:T(8,128)(2,1)S(1)}, u32[]{:S(2)}) copy-start(bf16[2,1024,1064]{1,2,0:T(8,128)(2,1)S(1)} %convolution_convert_fusion) | copy-start | bytes 13074436
  38.4 124.6 %collective-permute-start.6 = (bf16[2,3,512]{1,2,0:T(8,128)(2,1)}, bf16[2,3,512]{1,2,0:T(8,128)(2,1)S(1)}, u32[]{:S(2)}, u32[]{:S(2)}) collective-permute-start(bf16[2,3,512]{1,2,0:T(8,128)(2,1)} %get-tuple-element.450), channel_id=1, source_target_pairs={{0,4},{4,8},{8,12},{12,16},{16,20},{20,24},{24,28},{28,32},{32,36}... | collective-permute-start | bytes 18440 | tf_op jit(solution)/shard_map/ppermute | solution.py:52
  45.9 117.0 %collective-permute-start.7 = (bf16[2,3,512]{1,2,0:T(8,128)(2,1)}, bf16[2,3,512]{1,2,0:T(8,128)(2,1)S(1)}, u32[]{:S(2)}, u32[]{:S(2)}) collective-permute-start(bf16[2,3,512]{1,2,0:T(8,128)(2,1)} %get-tuple-element.449), channel_id=1, source_target_pairs={{4,0},{8,4},{12,8},{16,12},{20,16},{24,20},{28,24},{32,28},{36,32}... | collective-permute-start | bytes 18440 | tf_op jit(solution)/shard_map/ppermute | solution.py:54
  61.4 101.6 %slice-start = ((bf16[2,1024,1064]{1,2,0:T(8,128)(2,1)}), bf16[2,1024,512]{1,2,0:T(8,128)(2,1)S(1)}, s32[]{:S(2)}) async-start(bf16[2,1024,1064]{1,2,0:T(8,128)(2,1)} %copy-done.4), calls=%async_computation.2 | async-start | bytes 4194304 | tf_op jit(solution)/shard_map/slice | solution.py:153
  62.6 54.0 %copy-start.9 = (f32[2,8,8,128]{3,2,1,0:T(8,128)S(1)}, f32[2,8,8,128]{3,2,1,0:T(8,128)}, u32[]{:S(2)}) copy-start(f32[2,8,8,128]{3,2,1,0:T(8,128)} %add_exponential_fusion.1) | copy-start | bytes 196612
  287.8 230.9 %all-gather.9.cloned.1.call-start = ((), (), s32[]{:S(2)}) async-start(), calls=%async_computation | async-start | bytes 8519680 | tf_op jit(solution)/shard_map/all_gather | solution.py:19
  511.4 113.0 %copy-start.10 = (f32[2,8,1024]{2,1,0:T(8,128)S(1)}, f32[2,8,1024]{2,1,0:T(8,128)}, u32[]{:S(2)}) copy-start(f32[2,8,1024]{2,1,0:T(8,128)} %exp.105) | copy-start | bytes 196612
  634.7 99.0 %copy-start.7 = (bf16[1024,256]{1,0:T(8,128)(2,1)S(1)}, bf16[1024,256]{1,0:T(8,128)(2,1)}, u32[]{:S(2)}) copy-start(bf16[1024,256]{1,0:T(8,128)(2,1)} %copy-done.6) | copy-start | bytes 1572868
  634.7 100.0 %copy-start.1 = (bf16[256,1064]{0,1:T(8,128)(2,1)S(1)}, bf16[256,1064]{0,1:T(8,128)(2,1)}, u32[]{:S(2)}) copy-start(bf16[256,1064]{0,1:T(8,128)(2,1)} %param.19) | copy-start | bytes 1634308
  635.5 2.3 collective-permute-start.8
  637.8 13.4 %collective-permute-start.9 = (bf16[1024,256]{1,0:T(8,128)(2,1)S(1)}, bf16[1024,256]{1,0:T(8,128)(2,1)S(1)}, u32[]{:S(2)}, u32[]{:S(2)}) collective-permute-start(bf16[1024,256]{1,0:T(8,128)(2,1)S(1)} %collective-permute-done.8), channel_id=1, source_target_pairs={{0,8},{8,0},{4,12},{12,4},{16,24},{24,16},{20,28},{28,20},{32,40},... | collective-permute-start | bytes 1572872 | tf_op jit(solution)/shard_map/ppermute | solution.py:41
  651.2 25.9 %collective-permute-start.10 = (bf16[1024,256]{1,0:T(8,128)(2,1)S(1)}, bf16[1024,256]{1,0:T(8,128)(2,1)S(1)}, u32[]{:S(2)}, u32[]{:S(2)}) collective-permute-start(bf16[1024,256]{1,0:T(8,128)(2,1)S(1)} %collective-permute-done.9), channel_id=1, source_target_pairs={{0,16},{16,0},{4,20},{20,4},{8,24},{24,8},{12,28},{28,12},{32,48},... | collective-permute-start | bytes 1572872 | tf_op jit(solution)/shard_map/ppermute | solution.py:41
  677.1 28.4 %collective-permute-start.11 = (bf16[1024,256]{1,0:T(8,128)(2,1)S(1)}, bf16[1024,256]{1,0:T(8,128)(2,1)S(1)}, u32[]{:S(2)}, u32[]{:S(2)}) collective-permute-start(bf16[1024,256]{1,0:T(8,128)(2,1)S(1)} %collective-permute-done.10), channel_id=1, source_target_pairs={{0,32},{32,0},{4,36},{36,4},{8,40},{40,8},{12,44},{44,12},{16,48},... | collective-permute-start | bytes 1572872 | tf_op jit(solution)/shard_map/ppermute | solution.py:41
  705.5 13.0 %collective-permute-start.12 = (bf16[1024,256]{1,0:T(8,128)(2,1)S(1)}, bf16[1024,256]{1,0:T(8,128)(2,1)S(1)}, u32[]{:S(2)}, u32[]{:S(2)}) collective-permute-start(bf16[1024,256]{1,0:T(8,128)(2,1)S(1)} %collective-permute-done.11), channel_id=1, source_target_pairs={{0,64},{64,0},{4,68},{68,4},{8,72},{72,8},{12,76},{76,12},{16,80},... | collective-permute-start | bytes 1572872 | tf_op jit(solution)/shard_map/ppermute | solution.py:41
  718.5 13.3 %collective-permute-start.13 = (bf16[1024,256]{1,0:T(8,128)(2,1)S(1)}, bf16[1024,256]{1,0:T(8,128)(2,1)S(1)}, u32[]{:S(2)}, u32[]{:S(2)}) collective-permute-start(bf16[1024,256]{1,0:T(8,128)(2,1)S(1)} %collective-permute-done.12), channel_id=1, source_target_pairs={{0,128},{128,0},{4,132},{132,4},{8,136},{136,8},{12,140},{140,12},... | collective-permute-start | bytes 1572872 | tf_op jit(solution)/shard_map/ppermute | solution.py:41
  (5 other events, 17.7 us)
Sparse Core Ops, SparseCore 0:
  287.9 81.5 all-gather.10
  391.2 81.3 all-gather.8
where the time goes:
time: 753 us; the launch traced here: 742 us
  local copies, waits for them, and re-layouts  186 us (25%)
  matrix products  162 us (22%)
  other arithmetic  156 us (21%)
  waiting for transfers between devices  99.7 us (13%)
  blocking collectives  92.5 us (12%)
  starting transfers between devices  28.3 us (4%)
  between operations  13.8 us (2%)
    select_n x126, other arithmetic, hop(): jnp.where(position < mine, new, old)  125 us
    ppermute x12, waiting for transfers between devices, swapped(): return lax.ppermute(block, axis, route)  99.6 us
    all_gather x2, blocking collectives, carried_in(): pieces = jax.tree.map(lambda part: lax.all_gather(part, axis), value)  92.5 us
    mul x126, local copies, waits for them, and re-layouts, join_carry(): earlier[1] * later[0][:, :, None, None] + later[1]  83.3 us
    dot_general x16, matrix products, block_step(): jnp.einsum('trh,rhp->thp', scores[:, :, None] * decay, weighted, precisio...  64.6 us
    dot_general x16, matrix products, block_step(): jnp.einsum('rh,rhp,rn->hpn', tail, weighted, b_part, precision=highest)  31.6 us
    dot_general x16, matrix products, block_step(): jnp.einsum('tn,hpn->thp', c_part, state, precision=highest)  27.9 us
    squeeze x32, local copies, waits for them, and re-layouts, processor_sequence(): end_state, outputs = lax.scan(jax.vmap(block_step), init, pieces)  26.5 us
  transfers between devices with their start and end apart: 16, of which 11 were waited for; matrix products, arithmetic and copies ran while one was open for 34% of the time, Pallas kernels for 0%

commit v1 on v0

v1 whole, which is shorter than its diff:
```python
import functools

import jax
import jax.numpy as jnp
from jax import lax
from jax.experimental import pallas as pl
from jax.experimental.pallas import tpu as pltpu
from jax.sharding import PartitionSpec as P

D = 256
E = 512
NS = 16
KW = 4
H = 8
CH = 64
SB = 128
EPSILON = 1e-05
LOG2E = 1.4426950408889634
CHAINS = ((0, 0, False), (0, 1, True), (1, 0, True), (1, 1, False))
F32 = jnp.float32
BF16 = jnp.bfloat16


def split3(v):
    hi = v.astype(BF16)
    rest = v - hi.astype(F32)
    mid = rest.astype(BF16)
    lo = (rest - mid.astype(F32)).astype(BF16)
    return hi, mid, lo


def stack3(v):
    return jnp.concatenate(split3(v), axis=0)


def rounded(v):
    return lax.reduce_precision(v, exponent_bits=8, mantissa_bits=7)


def table3(v):
    hi = rounded(v)
    mid = rounded(v - hi)
    lo = v - hi - mid
    return jnp.concatenate([hi, mid, lo], axis=0).astype(BF16)


def dot(a, b):
    return jnp.dot(a, b, preferred_element_type=F32)


def onehots(taps_row):
    sym = lax.broadcasted_iota(jnp.int32, (8, SB), 0)
    return [(taps_row[j : j + 1, :] == sym).astype(F32) for j in range(8)]


def counts(center, backward):
    r = lax.broadcasted_iota(jnp.int32, (SB, SB), 0)
    c = lax.broadcasted_iota(jnp.int32, (SB, SB), 1)
    same = (r // CH) == (c // CH)
    keep = same & ((c >= r) if backward else (c <= r))
    return dot(keep.astype(BF16), center).astype(BF16)


def local_kernel(taps_ref, ct_ref, la_ref, dt_ref, s_ref, skip_ref, y_ref, u_ref, end_ref, dacc_ref, eacc_ref):
    step = pl.program_id(0)

    @pl.when(step == 0)
    def _():
        dacc_ref[...] = jnp.zeros_like(dacc_ref)
        eacc_ref[...] = jnp.zeros_like(eacc_ref)

    oht = onehots(taps_ref[...])
    oh = jnp.concatenate(oht, axis=0).T.astype(BF16)
    center = jnp.concatenate([oht[3]] * 16, axis=0).T.astype(BF16)
    center = center[:, :24]
    oh192 = jnp.concatenate([oh, oh, oh], axis=1)
    cnt = (counts(center, False), counts(center, True))

    lane = lax.broadcasted_iota(jnp.int32, (CH, SB), 1)
    row = lax.broadcasted_iota(jnp.int32, (CH, SB), 0)
    within = lane % CH
    diag = within == row
    low = lane < CH
    neg = (
        jnp.where(within <= row, 0.0, -1e30).astype(F32),
        jnp.where(within >= row, 0.0, -1e30).astype(F32),
    )
    lane8 = lax.broadcasted_iota(jnp.int32, (8, SB), 1)
    row8 = lax.broadcasted_iota(jnp.int32, (8, SB), 0)
    rolled = pltpu.roll(oht[3], CH, 1)
    ot2 = (jnp.where(lane8 < CH, oht[3], rolled), jnp.where(lane8 < CH, rolled, oht[3]))

    scores = []
    for strand in range(2):
        per_chunk = []
        for c in range(2):
            acc = None
            for b in range(5):
                term = s_ref[strand, b] * ot2[c][b : b + 1, :]
                acc = term if acc is None else acc + term
            per_chunk.append(dot(center[c * CH : (c + 1) * CH], stack3(acc)))
        scores.append(per_chunk)

    for n, (strand, k, backward) in enumerate(CHAINS):
        d = int(backward)
        for pair in range(4):
            cols = slice(n * E + pair * SB, n * E + (pair + 1) * SB)
            pre = dot(oh192, ct_ref[:, cols])
            xc = pre * jax.nn.sigmoid(pre)
            xw = xc * dot(center, dt_ref[:, cols])
            cum = dot(cnt[d], la_ref[:, cols])
            xh = xw.astype(BF16)
            xl = (xw - xh.astype(F32)).astype(BF16)
            for c in range(2):
                rows = slice(c * CH, (c + 1) * CH)
                cc = cum[rows]
                rowv = jnp.sum(jnp.where(diag, cc, 0.0), axis=0, keepdims=True)
                last = cc[0:1, :] if backward else cc[CH - 1 : CH, :]
                m = jnp.exp2(jnp.minimum(cc - rowv, neg[d])) * scores[strand][c]
                ext = jnp.exp2(jnp.minimum(last - rowv, 0.0)) * ot2[c]
                full = jnp.concatenate([m, ext, jnp.zeros_like(ext)], axis=0)
                mh = full.astype(BF16)
                ml = (full - mh.astype(F32)).astype(BF16)
                lhs = jnp.concatenate([mh, ml], axis=1)
                zero = jnp.zeros((CH, SB), BF16)
                top = jnp.concatenate([jnp.where(low, xh[rows], zero), jnp.where(low, xl[rows], zero)], axis=1)
                bot = jnp.concatenate([jnp.where(low, zero, xh[rows]), jnp.where(low, zero, xl[rows])], axis=1)
                rhs = jnp.concatenate([top, bot, top, bot], axis=0)
                out = dot(lhs, rhs)
                out = out[:, :SB] + out[:, SB:]
                y_ref[rows, cols] = out[:CH] + skip_ref[0:1, cols] * xc[rows]
                u = out[CH : CH + 8]
                ps = slice(pair * SB, (pair + 1) * SB)
                u_ref[c, n, :, ps] = jnp.where(row8 == 5, jnp.broadcast_to(last, (8, SB)), u)
                dacc = dacc_ref[n, 0:1, ps]
                eacc = eacc_ref[n, :, ps]
                if backward:
                    eacc = eacc + jnp.exp2(dacc) * u
                else:
                    eacc = eacc * jnp.exp2(last) + u
                dacc = dacc + last
                dacc_ref[n, 0:1, ps] = dacc
                eacc_ref[n, :, ps] = eacc
                end_ref[n, :, ps] = jnp.where(row8 == 5, jnp.broadcast_to(dacc, (8, SB)), eacc)


def finish_kernel(
    count, chunks, me_ref, taps_ref, la_ref, s_ref, gate_ref, gain_ref, emb_ref, wo_ref, u_ref, all_ref, y_ref,
    out_ref, in_ref
):
    step = pl.program_id(0)

    @pl.when(step == 0)
    def _():
        me = me_ref[0]
        for n, (strand, k, backward) in enumerate(CHAINS):

            def hop(i, s):
                j = count - 1 - i if backward else i
                piece = all_ref[j, n]
                use = (j > me) if backward else (j < me)
                return jnp.where(use, jnp.exp2(piece[5:6, :]) * s + piece, s)

            s = lax.fori_loop(0, count, hop, jnp.zeros((8, E), F32))

            def chunk(i, s):
                c = chunks - 1 - i if backward else i
                acc = None
                for b in range(5):
                    col = s_ref[strand, b]
                    term = jnp.concatenate([col] * 4, axis=1) * s[b : b + 1, :]
                    acc = term if acc is None else acc + term
                hi, mid, lo = split3(acc)
                in_ref[c, n] = jnp.concatenate(
                    [hi.astype(F32), mid.astype(F32), lo.astype(F32)], axis=0
                )
                piece = u_ref[c, n]
                return jnp.exp2(piece[5:6, :]) * s + piece

            lax.fori_loop(0, chunks, chunk, s)

    center = (
        taps_ref[3:4, :] == lax.broadcasted_iota(jnp.int32, (SB, SB), 0) % 8
    ).astype(F32).T.astype(BF16)[:, :24]
    cnt = (counts(center, False), counts(center, True))
    r = lax.broadcasted_iota(jnp.int32, (2 * SB, SB), 0)
    c = lax.broadcasted_iota(jnp.int32, (2 * SB, SB), 1)
    ones = (((r % SB) // CH) == (c // CH)).astype(BF16)

    total = dot(center[:, :8], emb_ref[...])
    for strand in range(2):
        mixed = []
        for pair in range(4):
            gate = dot(center, gate_ref[:, strand * E + pair * SB : strand * E + (pair + 1) * SB])
            ps = slice(pair * SB, (pair + 1) * SB)
            acc = None
            for k in range(2):
                n = strand * 2 + k
                backward = CHAINS[n][2]
                cols = slice(n * E + pair * SB, n * E + (pair + 1) * SB)
                reach = jnp.exp2(dot(cnt[int(backward)], la_ref[:, cols]))
                far = jnp.concatenate(
                    [
                        dot(center[h * CH : (h + 1) * CH], in_ref[step * 2 + h, n, :, ps].astype(BF16))
                        for h in range(2)
                    ],
                    axis=0,
                )
                g = (y_ref[:, cols] + reach * far) * gate
                sq = g * g
                sh = sq.astype(BF16)
                sl = (sq - sh.astype(F32)).astype(BF16)
                mean = dot(jnp.concatenate([sh, sl], axis=1), ones) * (1.0 / CH)
                normed = g * lax.rsqrt(mean + EPSILON) * gain_ref[k : k + 1, ps]
                acc = normed if acc is None else acc + normed
            mixed.append(acc.astype(BF16))
        strand_out = dot(jnp.concatenate(mixed, axis=1), wo_ref[strand])
        total = total + strand_out.astype(BF16).astype(F32)
    out_ref[...] = total.astype(BF16)


def per_device(
    token_ids,
    embed_table,
    input_weight_matrix,
    output_weight_matrix,
    conv_weight,
    dt_bias,
    decay_rate,
    skip_gain,
    norm_gain,
):
    rows = token_ids.shape[0]
    count = lax.axis_size("seq")
    blocks = rows // SB
    chunks = rows // CH
    rim = KW - 1

    edge = token_ids + 1
    left = lax.ppermute(edge[rows - rim :], "seq", [(i, i + 1) for i in range(count - 1)]) - 1
    right = lax.ppermute(edge[:rim], "seq", [(i + 1, i) for i in range(count - 1)]) - 1
    ext = jnp.concatenate([left, token_ids, right])
    taps = jnp.stack([ext[j : j + rows] for j in range(2 * rim + 1)] + [jnp.full((rows,), -1, jnp.int32)])

    both = jnp.stack([embed_table, embed_table[jnp.array([3, 2, 1, 0, 4])]])
    table = jnp.einsum("sad,df->saf", both, input_weight_matrix, preferred_element_type=F32)
    table = jnp.pad(rounded(table), ((0, 0), (0, 3), (0, 0)))
    gate = table[:, :, :E]
    values = table[:, :, E : 2 * E]
    b_part = table[:, :, 2 * E : 2 * E + NS]
    c_part = table[:, :, 2 * E + NS : 2 * E + 2 * NS]
    raw = table[:, :, 2 * E + 2 * NS :]

    conv_rows, dts, las = [], [], []
    for strand, k, backward in CHAINS:
        zero = jnp.zeros((8, E), F32)
        parts = []
        for j in range(8):
            tap = (2 * rim - j) if backward else j
            parts.append(conv_weight[k, tap][None, :] * values[strand] if 0 <= tap < KW else zero)
        conv_rows.append(jnp.concatenate(parts, axis=0))
        dt = jax.nn.softplus(raw[strand] + dt_bias[k][None, :])
        dts.append(jnp.repeat(dt, CH, axis=1))
        las.append(jnp.repeat(-decay_rate[k][None, :] * dt * LOG2E, CH, axis=1))
    ct = table3(jnp.concatenate(conv_rows, axis=1))
    dt3 = table3(jnp.concatenate(dts, axis=1))
    la3 = table3(jnp.concatenate(las, axis=1))
    gate3 = table3(jnp.concatenate(list(gate * jax.nn.sigmoid(gate)), axis=1))
    skip = jnp.concatenate([jnp.repeat(skip_gain[k], CH) for _, k, _ in CHAINS])[None, :]
    score = jnp.sum(c_part[:, :, None, :] * b_part[:, None, :, :], axis=-1)
    valid = (jnp.arange(8) < 5).astype(F32)
    score = score * valid[None, :, None] * valid[None, None, :]
    score = jnp.broadcast_to(jnp.swapaxes(score, 1, 2)[:, :, :, None], (2, 8, 8, SB))
    emb8 = jnp.pad(embed_table, ((0, 3), (0, 0)))
    wo = jnp.stack([output_weight_matrix, output_weight_matrix[:, ::-1]])

    whole = lambda shape: pl.BlockSpec(shape, lambda i: (0,) * len(shape))
    params = pltpu.CompilerParams(vmem_limit_bytes=56 * 1024 * 1024)
    y, u, end = pl.pallas_call(
        local_kernel,
        grid=(blocks,),
        out_shape=(
            jax.ShapeDtypeStruct((rows, 4 * E), F32),
            jax.ShapeDtypeStruct((chunks, 4, 8, E), F32),
            jax.ShapeDtypeStruct((4, 8, E), F32),
        ),
        in_specs=[
            pl.BlockSpec((8, SB), lambda i: (0, i)),
            whole((192, 4 * E)),
            whole((24, 4 * E)),
            whole((24, 4 * E)),
            whole((2, 8, 8, SB)),
            whole((1, 4 * E)),
        ],
        out_specs=(
            pl.BlockSpec((SB, 4 * E), lambda i: (i, 0)),
            pl.BlockSpec((2, 4, 8, E), lambda i: (i, 0, 0, 0)),
            whole((4, 8, E)),
        ),
        scratch_shapes=[pltpu.VMEM((4, 8, E), F32), pltpu.VMEM((4, 8, E), F32)],
        compiler_params=params,
        name="local_chunks",
    )(taps, ct, la3, dt3, score, skip)

    gathered = lax.all_gather(end, "seq")
    me = lax.axis_index("seq").astype(jnp.int32).reshape(1)
    return pl.pallas_call(
        functools.partial(finish_kernel, count, chunks),
        grid=(blocks,),
        out_shape=jax.ShapeDtypeStruct((rows, D), BF16),
        in_specs=[
            pl.BlockSpec(memory_space=pltpu.SMEM),
            pl.BlockSpec((8, SB), lambda i: (0, i)),
            whole((24, 4 * E)),
            whole((2, 8, 8, SB)),
            whole((24, 2 * E)),
            whole((2, E)),
            whole((8, D)),
            whole((2, E, D)),
            whole((chunks, 4, 8, E)),
            whole((count, 4, 8, E)),
            pl.BlockSpec((SB, 4 * E), lambda i: (i, 0)),
        ],
        out_specs=pl.BlockSpec((SB, D), lambda i: (i, 0)),
        scratch_shapes=[pltpu.VMEM((chunks, 4, 24, E), F32)],
        compiler_params=params,
        name="finish_rows",
    )(me, taps, la3, score, gate3, norm_gain, emb8, wo, u, gathered, y)


def solution(mesh):
    placed = (P(("batch", "seq")), P(), P(), P(), P(), P(), P(), P(), P())
    return jax.shard_map(
        per_device, mesh=mesh, in_specs=placed, out_specs=P(("batch", "seq"), None), check_vma=False
    )
```

time: 753 us -> 174 us (0.23); the launches traced: 742 us -> 174 us
  local copies, waits for them, and re-layouts: 186 us -> 7.47 us
  matrix products: 162 us -> 0.94 us
  other arithmetic: 156 us -> 7.17 us
  blocking collectives: 92.5 us -> 0 us
  Pallas kernels: 0 us -> 58.2 us
  starting transfers between devices: 28.3 us -> 7.06 us
  waiting for transfers between devices: 99.7 us -> 79.2 us
    dot_general x70 -> x1, matrix products: 162 us -> 0.94 us  [per_device(): jnp.einsum('sad,df->saf', both, input_weight_matrix, preferred_element_ty...]
    select_n x127 -> x0, other arithmetic: 125 us -> none  [the longest x126 125 us: hop(): jnp.where(position < mine, new, old)]
    ppermute x14 -> x2, waiting for transfers between devices: 99.6 us -> 0.01 us  [the longest x1 0.01 us: per_device(): lax.ppermute(edge[:rim], 'seq', [(i + 1, i) for i in range(count - 1)]) - 1]
    mul x144 -> x1, local copies, waits for them, and re-layouts: 94.8 us -> 0.07 us  [per_device(): score = score * valid[None, :, None] * valid[None, None, :]]
    all_gather x2 -> x0, blocking collectives: 92.5 us -> none  [carried_in(): pieces = jax.tree.map(lambda part: lax.all_gather(part, axis), value)]
    all_gather x2 -> x1, waiting for transfers between devices: 0.02 us -> 79.2 us  [per_device(): gathered = lax.all_gather(end, 'seq')]
    pallas_call x0 -> x2, Pallas kernels: none -> 58.2 us  [the longest x1 32.5 us: per_device(): pl.pallas_call(local_kernel, grid=(blocks,), out_shape=(jax.ShapeDtypeStr...]
    rev x10 -> x1, local copies, waits for them, and re-layouts: 27.2 us -> 0.83 us  [per_device(): wo = jnp.stack([output_weight_matrix, output_weight_matrix[:, ::-1]])]
  transfers between devices with their start and end apart: 16 -> 3, of which waited for: 11 -> 1; matrix products, arithmetic and copies ran while one was open for 34% -> 8% of each run, Pallas kernels for 0% -> 0%
where the time goes in v1:
time: 174 us
  waiting for transfers between devices  79.2 us (46%)
  Pallas kernels  58.2 us (33%)
  between operations  13.7 us (8%)
  local copies, waits for them, and re-layouts  7.47 us (4%)
  other arithmetic  7.17 us (4%)
  starting transfers between devices  7.06 us (4%)
    all_gather x1, waiting for transfers between devices, per_device(): gathered = lax.all_gather(end, 'seq')  79.2 us
    pallas_call x1, Pallas kernels, per_device(): pl.pallas_call(local_kernel, grid=(blocks,), out_shape=(jax.ShapeDtypeStr...  32.5 us
    pallas_call x1, Pallas kernels, per_device(): pl.pallas_call(functools.partial(finish_kernel, count, chunks), grid=(blo...  25.7 us
    ppermute x1, starting transfers between devices, per_device(): lax.ppermute(edge[:rim], 'seq', [(i + 1, i) for i in range(count - 1)]) - 1  5.14 us
  transfers between devices with their start and end apart: 3, of which 1 were waited for; matrix products, arithmetic and copies ran while one was open for 8% of the time, Pallas kernels for 0%

profile of v1, /device:TPU:1, one launch (start us, length us, event | category | flops | bytes accessed | tf_op | source)
XLA Modules:
  0.0 173.8 jit_solution(9296537421937799488)
XLA Ops:
  6.5 0.7 broadcast_add_fusion
  7.4 5.1 %collective-permute-start.1 = (s32[3]{0:T(128)S(1)}, s32[3]{0:T(128)S(1)}, u32[]{:S(2)}, u32[]{:S(2)}) collective-permute-start(s32[3]{0:T(128)S(1)} %get-tuple-element.68), channel_id=1, source_target_pairs={{4,0},{8,4},{12,8},{16,12},{20,16},{24,20},{28,24},{32,28},{36,32}... | collective-permute-start | bytes 44 | tf_op jit(solution)/shard_map/ppermute | solution.py:241
  12.5 1.9 %collective-permute-start = (s32[3]{0:T(128)S(1)}, s32[3]{0:T(128)S(1)}, u32[]{:S(2)}, u32[]{:S(2)}) collective-permute-start(s32[3]{0:T(128)S(1)} %get-tuple-element.69), channel_id=1, source_target_pairs={{0,4},{4,8},{8,12},{12,16},{16,20},{20,24},{24,28},{28,32},{32,36}... | collective-permute-start | bytes 44 | tf_op jit(solution)/shard_map/ppermute | solution.py:240
  14.5 0.8 slice_bitcast_fusion.3
  15.5 0.7 pad_clamp_fusion
  16.2 0.9 fusion.17
  17.1 1.2 gather_fusion
  18.3 0.9 convolution_reduce-precision_fusion
  19.4 0.1 multiply_reduce_fusion
  19.6 0.8 slice_bitcast_fusion.4
  22.0 0.6 pad_maximum_fusion.7
  22.6 0.6 pad_maximum_fusion.4.dt_ref
  23.3 0.6 pad_maximum_fusion.3.la_ref
  23.9 0.1 reduce-precision_convert_fusion.1
  24.1 1.0 pad_maximum_fusion.ct_ref
  25.2 0.7 stack.49.taps_ref
  25.9 0.7 broadcast_in_dim.53.s_ref
  26.6 32.5 %local_chunks.1 = (f32[1024,2048]{1,0:T(8,128)}, f32[16,4,8,512]{3,2,1,0:T(8,128)}, f32[4,8,512]{2,1,0:T(8,128)}) custom-call(s32[8,1024]{1,0:T(8,128)} %stack.49.taps_ref, bf16[192,2048]{1,0:T(8,128)(2,1)} %pad_maximum_fusion.ct_ref, bf16[24,2048]{1,0:T(8,128)(2,1)} %pad_maximum_fusion.3.la_ref, bf16[24,2048]{1,0:T(8,128)(2,1)} %pad_maximum_fusion.4.dt_ref, ...), custom_call_target="tpu_custom_call" | custom-call | tf_op jit(solution)/shard_map/local_chunks/pallas_call | solution.py:279
  59.1 0.6 pad.9.emb_ref
  59.7 0.8 rev.3
  60.6 0.6 pad_maximum_fusion.5.gate_ref
  61.2 0.9 pad_maximum_fusion.1.wo_ref
  62.1 79.2 %all-gather.3.cloned.1.call-done = f32[256,8,512]{2,1,0:T(8,128)} async-done(((f32[4,8,512]{2,1,0:T(8,128)}), f32[256,8,512]{2,1,0:T(8,128)}) %all-gather.3.cloned.1.call-update) | async-done | bytes 4194320 | tf_op jit(solution)/shard_map/all_gather | solution.py:305
  141.3 25.7 %finish_rows.1 = bf16[1024,256]{1,0:T(8,128)(2,1)} custom-call(s32[1]{0:T(128)} %bitcast.me_ref, s32[8,1024]{1,0:T(8,128)} %stack.49.taps_ref, bf16[24,2048]{1,0:T(8,128)(2,1)} %pad_maximum_fusion.3.la_ref, f32[2,8,8,128]{3,2,1,0:T(8,128)} %broadcast_in_dim.53.s_ref, bf16[24,1024]{1,0:T(8,128)(2,1)} %pad_maximum_fusion.5.gate_ref, f32[2,512]{1,0:T(2,128)} %gain_ref.1, ...), custom_call_target="tpu_custom_call" | custom-call | tf_op jit(solution)/shard_map/finish_rows/pallas_call | solution.py:307
  (71 shorter events, 2.2 us)
Async XLA Ops:
  6.5 11.8 %copy-start = (bf16[256,1064]{0,1:T(8,128)(2,1)S(1)}, bf16[256,1064]{0,1:T(8,128)(2,1)}, u32[]{:S(2)}) copy-start(bf16[256,1064]{0,1:T(8,128)(2,1)} %param.12) | copy-start | bytes 1634308
  6.5 134.8 %all-gather.3.cloned.1.call-start = ((), (), s32[]{:S(2)}) async-start(), calls=%async_computation | async-start | bytes 4259840 | tf_op jit(solution)/shard_map/all_gather | solution.py:305
  7.4 17.7 %collective-permute-start.1 = (s32[3]{0:T(128)S(1)}, s32[3]{0:T(128)S(1)}, u32[]{:S(2)}, u32[]{:S(2)}) collective-permute-start(s32[3]{0:T(128)S(1)} %get-tuple-element.68), channel_id=1, source_target_pairs={{4,0},{8,4},{12,8},{16,12},{20,16},{24,20},{28,24},{32,28},{36,32}... | collective-permute-start | bytes 44 | tf_op jit(solution)/shard_map/ppermute | solution.py:241
  12.5 12.6 %collective-permute-start = (s32[3]{0:T(128)S(1)}, s32[3]{0:T(128)S(1)}, u32[]{:S(2)}, u32[]{:S(2)}) collective-permute-start(s32[3]{0:T(128)S(1)} %get-tuple-element.69), channel_id=1, source_target_pairs={{0,4},{4,8},{8,12},{12,16},{16,20},{20,24},{24,28},{28,32},{32,36}... | collective-permute-start | bytes 44 | tf_op jit(solution)/shard_map/ppermute | solution.py:240
  23.3 1.8 %copy-start.3 = (s32[1024]{0:T(1024)S(1)}, s32[1024]{0:T(1024)}, u32[]{:S(2)}) copy-start(s32[1024]{0:T(1024)} %param.10) | copy-start | bytes 12292
  24.0 35.1 %copy-start.2 = (bf16[5,256]{1,0:T(8,128)(2,1)S(1)}, bf16[5,256]{1,0:T(8,128)(2,1)}, u32[]{:S(2)}) copy-start(bf16[5,256]{1,0:T(8,128)(2,1)} %param.11) | copy-start | bytes 7684
  24.1 35.7 %copy-start.1 = (bf16[512,256]{1,0:T(8,128)(2,1)S(1)}, bf16[512,256]{1,0:T(8,128)(2,1)}, u32[]{:S(2)}) copy-start(bf16[512,256]{1,0:T(8,128)(2,1)} %param.13) | copy-start | bytes 786436
Sparse Core Ops, SparseCore 0:
  59.2 82.0 all-gather.2

commit v2 on v1

--- a/solution.py
+++ b/solution.py
@@ -16,7 +16,10 @@
 SB = 128
 EPSILON = 1e-05
 LOG2E = 1.4426950408889634
-CHAINS = ((0, 0, False), (0, 1, True), (1, 0, True), (1, 1, False))
+CORES = 2
+NZ = 8
+CHAINS = ((0, 0, False), (1, 1, False), (0, 1, True), (1, 0, True))
+MESH = pl.DeviceIdType.MESH
 F32 = jnp.float32
 BF16 = jnp.bfloat16
 
@@ -31,17 +34,6 @@
 
 def stack3(v):
     return jnp.concatenate(split3(v), axis=0)
-
-
-def rounded(v):
-    return lax.reduce_precision(v, exponent_bits=8, mantissa_bits=7)
-
-
-def table3(v):
-    hi = rounded(v)
-    mid = rounded(v - hi)
-    lo = v - hi - mid
-    return jnp.concatenate([hi, mid, lo], axis=0).astype(BF16)
 
 
 def dot(a, b):
@@ -145,23 +137,13 @@
 
 
 def finish_kernel(
-    count, chunks, me_ref, taps_ref, la_ref, s_ref, gate_ref, gain_ref, emb_ref, wo_ref, u_ref, all_ref, y_ref,
-    out_ref, in_ref
+    chunks, taps_ref, la_ref, s_ref, gate_ref, gain_ref, emb_ref, wo_ref, u_ref, far_ref, y_ref, out_ref, in_ref
 ):
     step = pl.program_id(0)
 
     @pl.when(step == 0)
     def _():
-        me = me_ref[0]
         for n, (strand, k, backward) in enumerate(CHAINS):
-
-            def hop(i, s):
-                j = count - 1 - i if backward else i
-                piece = all_ref[j, n]
-                use = (j > me) if backward else (j < me)
-                return jnp.where(use, jnp.exp2(piece[5:6, :]) * s + piece, s)
-
-            s = lax.fori_loop(0, count, hop, jnp.zeros((8, E), F32))
 
             def chunk(i, s):
                 c = chunks - 1 - i if backward else i
@@ -177,7 +159,7 @@
                 piece = u_ref[c, n]
                 return jnp.exp2(piece[5:6, :]) * s + piece
 
-            lax.fori_loop(0, chunks, chunk, s)
+            lax.fori_loop(0, chunks, chunk, far_ref[int(backward), (n % 2) * 8 : (n % 2) * 8 + 8, :])
 
     center = (
         taps_ref[3:4, :] == lax.broadcasted_iota(jnp.int32, (SB, SB), 0) % 8
@@ -195,7 +177,7 @@
             ps = slice(pair * SB, (pair + 1) * SB)
             acc = None
             for k in range(2):
-                n = strand * 2 + k
+                n = [c[:2] for c in CHAINS].index((strand, k))
                 backward = CHAINS[n][2]
                 cols = slice(n * E + pair * SB, n * E + (pair + 1) * SB)
                 reach = jnp.exp2(dot(cnt[int(backward)], la_ref[:, cols]))
@@ -219,6 +201,145 @@
     out_ref[...] = total.astype(BF16)
 
 
+def greet(peers):
+    barrier = pltpu.get_barrier_semaphore()
+    for peer in peers:
+        pl.semaphore_signal(barrier, inc=1, device_id={"seq": peer}, device_id_type=MESH)
+    pl.semaphore_wait(barrier, len(peers))
+
+
+def tables_kernel(
+    count, tok_ref, emb_ref, w_ref, conv_ref, hp_ref, ct_ref, la_ref, dt_ref, gate_ref, s_ref, left_ref, right_ref,
+    halo_ref, send_sem, recv_sem
+):
+    me = lax.axis_index("seq")
+    up, down = lax.rem(me + 1, count), lax.rem(me + count - 1, count)
+    greet((up, down))
+    copies = [
+        pltpu.make_async_remote_copy(
+            src_ref=tok_ref.at[src], dst_ref=halo_ref.at[slot], send_sem=send_sem.at[slot],
+            recv_sem=recv_sem.at[slot], device_id={"seq": peer}, device_id_type=MESH,
+        )
+        for slot, src, peer in ((0, tok_ref.shape[0] - 1, up), (1, 0, down))
+    ]
+    for copy in copies:
+        copy.start()
+
+    sym = lax.broadcasted_iota(jnp.int32, (16, 5), 0)
+    col = lax.broadcasted_iota(jnp.int32, (16, 5), 1)
+    paired = jnp.where(sym < 8, sym, jnp.where(sym < 12, 11 - sym, sym - 8))
+    both = dot((paired == col).astype(BF16), emb_ref[...]).astype(BF16)
+    table = dot(both, w_ref[...]).astype(BF16)
+    gate = table[:, :E].astype(F32)
+    gate = gate * jax.nn.sigmoid(gate)
+    values = table[:, E : 2 * E].astype(F32)
+    tail = table[:, 2 * E :]
+    width = tail.shape[1]
+
+    def pick(first, cols, group):
+        r = lax.broadcasted_iota(jnp.int32, (width, cols), 0)
+        c = lax.broadcasted_iota(jnp.int32, (width, cols), 1)
+        return dot(tail, (r - first == c // group).astype(BF16))
+
+    raw = pick(2 * NS, E, CH)
+    b_part, c_part = pick(0, NS, 1), pick(NS, NS, 1)
+    for strand in range(2):
+        at = slice(strand * 8, strand * 8 + 8)
+        gate_ref[:, strand * E : (strand + 1) * E] = stack3(gate[at])
+        for b in range(8):
+            row = b_part[strand * 8 + b : strand * 8 + b + 1, :]
+            s_ref[strand, b] = jnp.broadcast_to(jnp.sum(c_part[at] * row, axis=1, keepdims=True), (8, SB))
+    for n, (strand, k, backward) in enumerate(CHAINS):
+        at = slice(strand * 8, strand * 8 + 8)
+        cols = slice(n * E, (n + 1) * E)
+        zero = jnp.zeros((8, E), F32)
+        parts = []
+        for j in range(8):
+            tap = (2 * (KW - 1) - j) if backward else j
+            parts.append(conv_ref[k, tap : tap + 1, :] * values[at] if 0 <= tap < KW else zero)
+        ct_ref[:, cols] = stack3(jnp.concatenate(parts, axis=0))
+        dt = jax.nn.softplus(raw[at] + hp_ref[k : k + 1, :])
+        dt_ref[:, cols] = stack3(dt)
+        la_ref[:, cols] = stack3(-hp_ref[2 + k : 3 + k, :] * dt * LOG2E)
+
+    for copy in copies:
+        copy.wait()
+    left_ref[...] = halo_ref[0]
+    right_ref[...] = halo_ref[1]
+
+
+def compose(earlier, later):
+    row = lax.broadcasted_iota(jnp.int32, (8, E), 0)
+    parts = []
+    for i in range(2):
+        e, l = earlier[8 * i : 8 * i + 8], later[8 * i : 8 * i + 8]
+        parts.append(jnp.where(row == 5, 1.0, jnp.exp2(l[5:6, :])) * e + l)
+    return jnp.concatenate(parts, axis=0)
+
+
+def scan_kernel(
+    count, end_ref, in_ref, pair_ref, back_ref, chip_ref, z_ref, line_ref, y_ref, other_ref, send_sem, recv_sem,
+    zsend_sem, zrecv_sem, ysend_sem, yrecv_sem
+):
+    nz, ny = NZ, count // (NZ * CORES)
+    me = lax.axis_index("seq")
+    core = lax.rem(me, CORES)
+    z = lax.rem(me // CORES, nz)
+    y = me // (CORES * nz)
+    sign = 1 - 2 * core
+    pz = z * sign + core * (nz - 1)
+    py = y * sign + core * (ny - 1)
+    partner = me + sign
+    zpeers = [(y * nz + lax.rem(z + d * sign + nz, nz)) * CORES + core for d in range(1, nz)]
+    ypeers = [(lax.rem(y + d * sign + ny, ny) * nz + z) * CORES + core for d in range(1, ny)]
+    greet([partner] + zpeers + ypeers)
+
+    def remote(src, dst, send, recv, peer):
+        return pltpu.make_async_remote_copy(
+            src_ref=src, dst_ref=dst, send_sem=send, recv_sem=recv, device_id={"seq": peer}, device_id_type=MESH
+        )
+
+    def merge(position, size, slots_ref, mine):
+        before = jnp.zeros_like(mine)
+        for d in range(size - 1, 0, -1):
+            before = jnp.where(d <= position, compose(before, slots_ref[d - 1]), before)
+        total = compose(before, mine)
+        for d in range(size - 1, 0, -1):
+            total = jnp.where(d > position, compose(total, slots_ref[d - 1]), total)
+        return before, total
+
+    copy = remote(end_ref.at[1 - core], pair_ref, send_sem.at[0], recv_sem.at[0], partner)
+    copy.start()
+    copy.wait()
+    mine = end_ref[core]
+    chip = compose(mine, pair_ref[...])
+    chip_ref[...] = chip
+    copies = [
+        remote(chip_ref, z_ref.at[d], zsend_sem.at[d], zrecv_sem.at[d], peer) for d, peer in enumerate(zpeers)
+    ]
+    for copy in copies:
+        copy.start()
+    for copy in copies:
+        copy.wait()
+    before, line = merge(pz, nz, z_ref, chip)
+    line_ref[...] = line
+    copies = [
+        remote(line_ref, y_ref.at[d], ysend_sem.at[d], yrecv_sem.at[d], peer) for d, peer in enumerate(ypeers)
+    ]
+    for copy in copies:
+        copy.start()
+    for copy in copies:
+        copy.wait()
+    far, _ = merge(py, ny, y_ref, line)
+    incoming = compose(far, before)
+    other_ref[...] = compose(incoming, mine)
+    copy = remote(other_ref, back_ref, send_sem.at[1], recv_sem.at[1], partner)
+    copy.start()
+    copy.wait()
+    in_ref[core] = incoming
+    in_ref[1 - core] = back_ref[...]
+
+
 def per_device(
     token_ids,
     embed_table,
@@ -236,43 +357,37 @@
     chunks = rows // CH
     rim = KW - 1
 
-    edge = token_ids + 1
-    left = lax.ppermute(edge[rows - rim :], "seq", [(i, i + 1) for i in range(count - 1)]) - 1
-    right = lax.ppermute(edge[:rim], "seq", [(i + 1, i) for i in range(count - 1)]) - 1
+    hp = jnp.concatenate([jnp.repeat(v, CH, axis=1) for v in (dt_bias, decay_rate, skip_gain)])
+    skip = jnp.concatenate([hp[4 + k] for _, k, _ in CHAINS])[None, :]
+    emb8 = jnp.pad(embed_table, ((0, 3), (0, 0)))
+    wo = jnp.stack([output_weight_matrix, output_weight_matrix[:, ::-1]])
+    vmem = pl.BlockSpec(memory_space=pltpu.VMEM)
+
+    token_rows = token_ids.reshape(rows // SB, 1, SB)
+    ct, la3, dt3, gate3, score, left, right = pl.pallas_call(
+        functools.partial(tables_kernel, count),
+        out_shape=(
+            jax.ShapeDtypeStruct((192, 4 * E), BF16),
+            jax.ShapeDtypeStruct((24, 4 * E), BF16),
+            jax.ShapeDtypeStruct((24, 4 * E), BF16),
+            jax.ShapeDtypeStruct((24, 2 * E), BF16),
+            jax.ShapeDtypeStruct((2, 8, 8, SB), F32),
+            jax.ShapeDtypeStruct((1, SB), jnp.int32),
+            jax.ShapeDtypeStruct((1, SB), jnp.int32),
+        ),
+        in_specs=[vmem] * 5,
+        out_specs=(vmem,) * 7,
+        scratch_shapes=[
+            pltpu.VMEM((2, 1, SB), jnp.int32), pltpu.SemaphoreType.DMA((2,)), pltpu.SemaphoreType.DMA((2,))
+        ],
+        compiler_params=pltpu.CompilerParams(collective_id=0, has_side_effects=True),
+        name="tables",
+    )(token_rows, embed_table, input_weight_matrix, conv_weight, hp)
+    me = lax.axis_index("seq")
+    left = jnp.where(me > 0, left[0, SB - rim :], -1)
+    right = jnp.where(me < count - 1, right[0, :rim], -1)
     ext = jnp.concatenate([left, token_ids, right])
     taps = jnp.stack([ext[j : j + rows] for j in range(2 * rim + 1)] + [jnp.full((rows,), -1, jnp.int32)])
-
-    both = jnp.stack([embed_table, embed_table[jnp.array([3, 2, 1, 0, 4])]])
-    table = jnp.einsum("sad,df->saf", both, input_weight_matrix, preferred_element_type=F32)
-    table = jnp.pad(rounded(table), ((0, 0), (0, 3), (0, 0)))
-    gate = table[:, :, :E]
-    values = table[:, :, E : 2 * E]
-    b_part = table[:, :, 2 * E : 2 * E + NS]
-    c_part = table[:, :, 2 * E + NS : 2 * E + 2 * NS]
-    raw = table[:, :, 2 * E + 2 * NS :]
-
-    conv_rows, dts, las = [], [], []
-    for strand, k, backward in CHAINS:
-        zero = jnp.zeros((8, E), F32)
-        parts = []
-        for j in range(8):
-            tap = (2 * rim - j) if backward else j
-            parts.append(conv_weight[k, tap][None, :] * values[strand] if 0 <= tap < KW else zero)
-        conv_rows.append(jnp.concatenate(parts, axis=0))
-        dt = jax.nn.softplus(raw[strand] + dt_bias[k][None, :])
-        dts.append(jnp.repeat(dt, CH, axis=1))
-        las.append(jnp.repeat(-decay_rate[k][None, :] * dt * LOG2E, CH, axis=1))
-    ct = table3(jnp.concatenate(conv_rows, axis=1))
-    dt3 = table3(jnp.concatenate(dts, axis=1))
-    la3 = table3(jnp.concatenate(las, axis=1))
-    gate3 = table3(jnp.concatenate(list(gate * jax.nn.sigmoid(gate)), axis=1))
-    skip = jnp.concatenate([jnp.repeat(skip_gain[k], CH) for _, k, _ in CHAINS])[None, :]
-    score = jnp.sum(c_part[:, :, None, :] * b_part[:, None, :, :], axis=-1)
-    valid = (jnp.arange(8) < 5).astype(F32)
-    score = score * valid[None, :, None] * valid[None, None, :]
-    score = jnp.broadcast_to(jnp.swapaxes(score, 1, 2)[:, :, :, None], (2, 8, 8, SB))
-    emb8 = jnp.pad(embed_table, ((0, 3), (0, 0)))
-    wo = jnp.stack([output_weight_matrix, output_weight_matrix[:, ::-1]])
 
     whole = lambda shape: pl.BlockSpec(shape, lambda i: (0,) * len(shape))
     params = pltpu.CompilerParams(vmem_limit_bytes=56 * 1024 * 1024)
@@ -302,14 +417,31 @@
         name="local_chunks",
     )(taps, ct, la3, dt3, score, skip)
 
-    gathered = lax.all_gather(end, "seq")
-    me = lax.axis_index("seq").astype(jnp.int32).reshape(1)
+    nz, ny = NZ, count // (NZ * CORES)
+    state = pltpu.VMEM((16, E), F32)
+    far = pl.pallas_call(
+        functools.partial(scan_kernel, count),
+        out_shape=jax.ShapeDtypeStruct((2, 16, E), F32),
+        in_specs=[vmem],
+        out_specs=vmem,
+        scratch_shapes=[
+            state,
+            state,
+            state,
+            pltpu.VMEM((max(nz - 1, 1), 16, E), F32),
+            state,
+            pltpu.VMEM((max(ny - 1, 1), 16, E), F32),
+            state,
+        ]
+        + [pltpu.SemaphoreType.DMA((max(m, 1),)) for m in (2, 2, nz - 1, nz - 1, ny - 1, ny - 1)],
+        compiler_params=pltpu.CompilerParams(collective_id=1, has_side_effects=True),
+        name="state_scan",
+    )(end.reshape(2, 16, E))
     return pl.pallas_call(
-        functools.partial(finish_kernel, count, chunks),
+        functools.partial(finish_kernel, chunks),
         grid=(blocks,),
         out_shape=jax.ShapeDtypeStruct((rows, D), BF16),
         in_specs=[
-            pl.BlockSpec(memory_space=pltpu.SMEM),
             pl.BlockSpec((8, SB), lambda i: (0, i)),
             whole((24, 4 * E)),
             whole((2, 8, 8, SB)),
@@ -318,14 +450,14 @@
             whole((8, D)),
             whole((2, E, D)),
             whole((chunks, 4, 8, E)),
-            whole((count, 4, 8, E)),
+            whole((2, 16, E)),
             pl.BlockSpec((SB, 4 * E), lambda i: (i, 0)),
         ],
         out_specs=pl.BlockSpec((SB, D), lambda i: (i, 0)),
         scratch_shapes=[pltpu.VMEM((chunks, 4, 24, E), F32)],
         compiler_params=params,
         name="finish_rows",
-    )(me, taps, la3, score, gate3, norm_gain, emb8, wo, u, gathered, y)
+    )(taps, la3, score, gate3, norm_gain, emb8, wo, u, far, y)
 
 
 def solution(mesh):

time: 174 us -> 103 us (0.59)
  waiting for transfers between devices: 79.2 us -> 0 us
  Pallas kernels: 58.2 us -> 85.5 us
  between operations: 13.7 us -> 0.06 us
  starting transfers between devices: 7.06 us -> 0 us
  local copies, waits for them, and re-layouts: 7.47 us -> 11.8 us
  other arithmetic: 7.17 us -> 4.73 us
    all_gather x1 -> x0, waiting for transfers between devices: 79.2 us -> none  [per_device(): gathered = lax.all_gather(end, 'seq')]
    pallas_call x1 -> x3, Pallas kernels: 25.7 us -> 53.1 us  [the longest x1 21.3 us: per_device(): pl.pallas_call(functools.partial(finish_kernel, chunks), grid=(blocks,),...]
    ppermute x2 -> x0, starting transfers between devices: 7.06 us -> none  [the longest x1 5.14 us: per_device(): lax.ppermute(edge[:rim], 'seq', [(i + 1, i) for i in range(count - 1)]) - 1]
    rev x1, local copies, waits for them, and re-layouts: 0.83 us -> 3.52 us  [per_device(): wo = jnp.stack([output_weight_matrix, output_weight_matrix[:, ::-1]])]
    concatenate x5 -> x2, other arithmetic: 3.52 us -> 1.23 us  [the longest x1 0.62 us: per_device(): jnp.concatenate([jnp.repeat(v, CH, axis=1) for v in (dt_bias, decay_rate,...]
    unnamed x15 -> x1, local copies, waits for them, and re-layouts: 0.05 us -> 2.12 us
  transfers between devices with their start and end apart: 3 -> 0, of which waited for: 1 -> 0; matrix products, arithmetic and copies ran while one was open for 8% -> 0% of each run, Pallas kernels for 0% -> 0%
where the time goes in v2:
time: 103 us; the launch traced here: 102 us
  Pallas kernels  85.5 us (83%)
  local copies, waits for them, and re-layouts  11.8 us (11%)
  other arithmetic  4.73 us (5%)
    pallas_call x1, Pallas kernels, per_device(): pl.pallas_call(local_kernel, grid=(blocks,), out_shape=(jax.ShapeDtypeStr...  32.4 us
    pallas_call x1, Pallas kernels, per_device(): pl.pallas_call(functools.partial(finish_kernel, chunks), grid=(blocks,),...  21.3 us
    pallas_call x1, Pallas kernels, per_device(): pl.pallas_call(functools.partial(scan_kernel, count), out_shape=jax.Shape...  19.9 us
    pallas_call x1, Pallas kernels, per_device(): pl.pallas_call(functools.partial(tables_kernel, count), out_shape=(jax.Sh...  12 us
    rev x1, local copies, waits for them, and re-layouts, per_device(): wo = jnp.stack([output_weight_matrix, output_weight_matrix[:, ::-1]])  3.52 us
    broadcast_in_dim x7, local copies, waits for them, and re-layouts, per_device(): jnp.repeat(v, CH, axis=1)  2.54 us
    unnamed x1, local copies, waits for them, and re-layouts  2.12 us

profile of v2, /device:TPU:1, one launch (start us, length us, event | category | flops | bytes accessed | tf_op | source)
XLA Modules:
  0.0 102.1 jit_solution(17452086422184983266)
XLA Ops:
  0.0 2.1 %copy.10.w_ref = bf16[256,1064]{1,0:T(8,128)(2,1)} copy(bf16[256,1064]{0,1:T(8,128)(2,1)} %param.11) | data formatting | bytes 1089536 | tf_op args[2]
  2.1 0.7 broadcast_in_dim.25
  2.9 0.1 reshape.30
  2.9 0.7 broadcast_in_dim.26
  3.7 0.1 reshape.31
  3.8 0.7 broadcast_in_dim.27
  4.5 0.1 reshape.32
  4.6 0.6 pad_maximum_fusion.1.hp_ref
  5.2 12.0 %tables.1 = (bf16[192,2048]{1,0:T(8,128)(2,1)}, bf16[24,2048]{1,0:T(8,128)(2,1)}, bf16[24,2048]{1,0:T(8,128)(2,1)}, bf16[24,1024]{1,0:T(8,128)(2,1)}, f32[2,8,8,...) custom-call(s32[8,1,128]{2,1,0:T(1,128)} %bitcast.23, bf16[5,256]{1,0:T(8,128)(2,1)} %emb_ref.1, ...), custom_call_target="tpu_custom_call" | custom-call | tf_op jit(solution)/shard_map/tables/pallas_call | solution.py:367
  17.2 0.7 fusion.4
  18.0 1.0 pad_add_fusion
  19.0 1.3 %stack.40.taps_ref = s32[8,1024]{1,0:T(8,128)} concatenate(s32[1,1024]{1,0:T(1,128)S(1)} %bitcast.30, s32[1,1024]{1,0:T(1,128)S(1)} %bitcast.29, s32[1,1024]{1,0:T(1,128)S(1)} %bitcast.31, s32[1,1024]{1,0:T(1,128)} %bitcast.24, s32[1,1024]{1,0:T(1,128)S(1)} %bitcast.27, s32[1,1024]{1,0:T(1,128)S(1)} %bitcast.28, s32[1,1024]{1,0:T(1,128)S(1)} %bitcast.26, ...), dimensions={0} | concatenate | bytes 65536 | tf_op jit(solution)/shard_map/stack | solution.py:390
  20.3 0.8 slice_bitcast_fusion
  21.1 0.1 broadcast_in_dim.29
  21.1 0.1 broadcast_in_dim.30
  21.2 0.1 broadcast_in_dim.31
  21.3 0.1 broadcast_in_dim.32
  21.4 0.6 pad_maximum_fusion.2
  22.0 32.4 %local_chunks.1 = (f32[1024,2048]{1,0:T(8,128)}, f32[16,4,8,512]{3,2,1,0:T(8,128)}, f32[4,8,512]{2,1,0:T(8,128)}) custom-call(s32[8,1024]{1,0:T(8,128)} %stack.40.taps_ref, bf16[192,2048]{1,0:T(8,128)(2,1)} %get-tuple-element.20.ct_ref, bf16[24,2048]{1,0:T(8,128)(2,1)} %get-tuple-element.17.la_ref, bf16[24,2048]{1,0:T(8,128)(2,1)} %get-tuple-element.21.dt_ref, ...), custom_call_target="tpu_custom_call" | custom-call | tf_op jit(solution)/shard_map/local_chunks/pallas_call | solution.py:394
  54.3 19.9 %state_scan.1.far_ref = f32[2,16,512]{2,1,0:T(8,128)} custom-call(f32[2,16,512]{2,1,0:T(8,128)} %bitcast.22), custom_call_target="tpu_custom_call" | custom-call | tf_op jit(solution)/shard_map/state_scan/pallas_call | solution.py:422
  74.2 3.5 %rev.3 = bf16[512,256]{1,0:T(8,128)(2,1)S(1)} reverse(bf16[512,256]{1,0:T(8,128)(2,1)} %param.12), dimensions={1} | reverse | bytes 524288 | tf_op jit(solution)/shard_map/rev | solution.py:363
  77.7 1.8 %pad_maximum_fusion.wo_ref = bf16[2,512,256]{2,1,0:T(8,128)(2,1)} fusion(bf16[1,512,256]{2,1,0:T(8,128)(2,1)S(1)} %bitcast.21, bf16[1,512,256]{2,1,0:T(8,128)(2,1)} %bitcast.20), kind=kLoop, calls=%fused_computation | loop fusion | flops 262144 | bytes 1048576 | tf_op jit(solution)/shard_map/stack | solution.py:363
  79.5 1.3 %pad.4.emb_ref = bf16[8,256]{1,0:T(8,128)(2,1)} pad(bf16[5,256]{1,0:T(8,128)(2,1)} %emb_ref.1, bf16[]{:T(256)} %constant.14.clone.1), padding=0_3x0_0 | pad | bytes 6658 | tf_op jit(solution)/shard_map/jit(_pad)/pad | solution.py:362
  80.8 21.3 %finish_rows.1 = bf16[1024,256]{1,0:T(8,128)(2,1)} custom-call(s32[8,1024]{1,0:T(8,128)} %stack.40.taps_ref, bf16[24,2048]{1,0:T(8,128)(2,1)} %get-tuple-element.17.la_ref, f32[2,8,8,128]{3,2,1,0:T(8,128)} %get-tuple-element.18.s_ref, bf16[24,1024]{1,0:T(8,128)(2,1)} %get-tuple-element.19.gate_ref, f32[2,512]{1,0:T(2,128)} %gain_ref.1, ...), custom_call_target="tpu_custom_call" | custom-call | tf_op jit(solution)/shard_map/finish_rows/pallas_call | solution.py:440
  (1 shorter events, 0.0 us)

commit v3 on v2

--- a/solution.py
+++ b/solution.py
@@ -53,7 +53,7 @@
     return dot(keep.astype(BF16), center).astype(BF16)
 
 
-def local_kernel(taps_ref, ct_ref, la_ref, dt_ref, s_ref, skip_ref, y_ref, u_ref, end_ref, dacc_ref, eacc_ref):
+def local_kernel(taps_ref, tab_ref, s_ref, skip_ref, y_ref, u_ref, end_ref, dacc_ref, eacc_ref):
     step = pl.program_id(0)
 
     @pl.when(step == 0)
@@ -63,10 +63,9 @@
 
     oht = onehots(taps_ref[...])
     oh = jnp.concatenate(oht, axis=0).T.astype(BF16)
-    center = jnp.concatenate([oht[3]] * 16, axis=0).T.astype(BF16)
+    center = jnp.concatenate([oht[3]] * 3 + [jnp.zeros_like(oht[3])] * 5, axis=0).T.astype(BF16)
+    keys = [jnp.concatenate([oh, oh, oh, counts(center, backward)], axis=1) for backward in (False, True)]
     center = center[:, :24]
-    oh192 = jnp.concatenate([oh, oh, oh], axis=1)
-    cnt = (counts(center, False), counts(center, True))
 
     lane = lax.broadcasted_iota(jnp.int32, (CH, SB), 1)
     row = lax.broadcasted_iota(jnp.int32, (CH, SB), 0)
@@ -97,10 +96,12 @@
         d = int(backward)
         for pair in range(4):
             cols = slice(n * E + pair * SB, n * E + (pair + 1) * SB)
-            pre = dot(oh192, ct_ref[:, cols])
+            base = (n * 4 + pair) * 3 * SB
+            found = dot(keys[d], tab_ref[:, base : base + 3 * SB])
+            pre = found[:, :SB]
             xc = pre * jax.nn.sigmoid(pre)
-            xw = xc * dot(center, dt_ref[:, cols])
-            cum = dot(cnt[d], la_ref[:, cols])
+            xw = xc * found[:, SB : 2 * SB]
+            cum = found[:, 2 * SB :]
             xh = xw.astype(BF16)
             xl = (xw - xh.astype(F32)).astype(BF16)
             for c in range(2):
@@ -137,12 +138,16 @@
 
 
 def finish_kernel(
-    chunks, taps_ref, la_ref, s_ref, gate_ref, gain_ref, emb_ref, wo_ref, u_ref, far_ref, y_ref, out_ref, in_ref
+    chunks, taps_ref, la_ref, s_ref, gate_ref, gain_ref, emb_ref, wo_ref, u_ref, far_ref, y_ref, out_ref, in_ref,
+    rev_ref
 ):
     step = pl.program_id(0)
 
     @pl.when(step == 0)
     def _():
+        r = lax.broadcasted_iota(jnp.int32, (D, D), 0)
+        c = lax.broadcasted_iota(jnp.int32, (D, D), 1)
+        rev_ref[...] = dot(wo_ref[...], (r + c == D - 1).astype(BF16)).astype(BF16)
         for n, (strand, k, backward) in enumerate(CHAINS):
 
             def chunk(i, s):
@@ -169,17 +174,17 @@
     c = lax.broadcasted_iota(jnp.int32, (2 * SB, SB), 1)
     ones = (((r % SB) // CH) == (c // CH)).astype(BF16)
 
-    total = dot(center[:, :8], emb_ref[...])
+    total = dot(center[:, :5], emb_ref[...])
     for strand in range(2):
         mixed = []
-        for pair in range(4):
-            gate = dot(center, gate_ref[:, strand * E + pair * SB : strand * E + (pair + 1) * SB])
-            ps = slice(pair * SB, (pair + 1) * SB)
+        for half in range(2):
+            ps = slice(half * 2 * SB, (half + 1) * 2 * SB)
+            gate = dot(center, gate_ref[:, strand * E + half * 2 * SB : strand * E + (half + 1) * 2 * SB])
             acc = None
             for k in range(2):
                 n = [c[:2] for c in CHAINS].index((strand, k))
                 backward = CHAINS[n][2]
-                cols = slice(n * E + pair * SB, n * E + (pair + 1) * SB)
+                cols = slice(n * E + half * 2 * SB, n * E + (half + 1) * 2 * SB)
                 reach = jnp.exp2(dot(cnt[int(backward)], la_ref[:, cols]))
                 far = jnp.concatenate(
                     [
@@ -192,11 +197,17 @@
                 sq = g * g
                 sh = sq.astype(BF16)
                 sl = (sq - sh.astype(F32)).astype(BF16)
-                mean = dot(jnp.concatenate([sh, sl], axis=1), ones) * (1.0 / CH)
+                mean = jnp.concatenate(
+                    [
+                        dot(jnp.concatenate([sh[:, q * SB : (q + 1) * SB], sl[:, q * SB : (q + 1) * SB]], axis=1), ones)
+                        for q in range(2)
+                    ],
+                    axis=1,
+                ) * (1.0 / CH)
                 normed = g * lax.rsqrt(mean + EPSILON) * gain_ref[k : k + 1, ps]
                 acc = normed if acc is None else acc + normed
             mixed.append(acc.astype(BF16))
-        strand_out = dot(jnp.concatenate(mixed, axis=1), wo_ref[strand])
+        strand_out = dot(jnp.concatenate(mixed, axis=1), (rev_ref if strand else wo_ref)[...])
         total = total + strand_out.astype(BF16).astype(F32)
     out_ref[...] = total.astype(BF16)
 
@@ -209,8 +220,8 @@
 
 
 def tables_kernel(
-    count, tok_ref, emb_ref, w_ref, conv_ref, hp_ref, ct_ref, la_ref, dt_ref, gate_ref, s_ref, left_ref, right_ref,
-    halo_ref, send_sem, recv_sem
+    count, tok_ref, emb_ref, w_ref, conv_ref, bias_ref, rate_ref, gain_ref, tab_ref, la_ref, gate_ref, s_ref,
+    skip_ref, taps_ref, halo_ref, send_sem, recv_sem
 ):
     me = lax.axis_index("seq")
     up, down = lax.rem(me + 1, count), lax.rem(me + count - 1, count)
@@ -229,7 +240,9 @@
     col = lax.broadcasted_iota(jnp.int32, (16, 5), 1)
     paired = jnp.where(sym < 8, sym, jnp.where(sym < 12, 11 - sym, sym - 8))
     both = dot((paired == col).astype(BF16), emb_ref[...]).astype(BF16)
-    table = dot(both, w_ref[...]).astype(BF16)
+    table = lax.dot_general(
+        both, w_ref[...], (((1,), (1,)), ((), ())), preferred_element_type=F32
+    ).astype(BF16)
     gate = table[:, :E].astype(F32)
     gate = gate * jax.nn.sigmoid(gate)
     values = table[:, E : 2 * E].astype(F32)
@@ -249,23 +262,60 @@
         for b in range(8):
             row = b_part[strand * 8 + b : strand * 8 + b + 1, :]
             s_ref[strand, b] = jnp.broadcast_to(jnp.sum(c_part[at] * row, axis=1, keepdims=True), (8, SB))
+    spread = (
+        lax.broadcasted_iota(jnp.int32, (H, E), 0) == lax.broadcasted_iota(jnp.int32, (H, E), 1) // CH
+    ).astype(BF16)
+
+    def widen(v):
+        hi, mid, lo = split3(v)
+        return dot(hi, spread) + dot(mid, spread) + dot(lo, spread)
+
+    bias, rate, skip = widen(bias_ref[...]), widen(rate_ref[...]), widen(gain_ref[...])
     for n, (strand, k, backward) in enumerate(CHAINS):
         at = slice(strand * 8, strand * 8 + 8)
-        cols = slice(n * E, (n + 1) * E)
         zero = jnp.zeros((8, E), F32)
         parts = []
         for j in range(8):
             tap = (2 * (KW - 1) - j) if backward else j
             parts.append(conv_ref[k, tap : tap + 1, :] * values[at] if 0 <= tap < KW else zero)
-        ct_ref[:, cols] = stack3(jnp.concatenate(parts, axis=0))
-        dt = jax.nn.softplus(raw[at] + hp_ref[k : k + 1, :])
-        dt_ref[:, cols] = stack3(dt)
-        la_ref[:, cols] = stack3(-hp_ref[2 + k : 3 + k, :] * dt * LOG2E)
+        conv = stack3(jnp.concatenate(parts, axis=0))
+        dt = jax.nn.softplus(raw[at] + bias[k : k + 1, :])
+        steps = []
+        for part in split3(dt):
+            steps += [zero] * 3 + [part.astype(F32)] + [zero] * 4
+        steps = jnp.concatenate(steps, axis=0).astype(BF16)
+        la = [part.astype(F32) for part in split3(-rate[k : k + 1, :] * dt * LOG2E)]
+        la_ref[:, n * E : (n + 1) * E] = jnp.concatenate(la, axis=0).astype(BF16)
+        la = jnp.concatenate(la + [zero] * 5, axis=0).astype(BF16)
+        for pair in range(4):
+            ps = slice(pair * SB, (pair + 1) * SB)
+            base = (n * 4 + pair) * 3 * SB
+            tab_ref[0:192, base : base + SB] = conv[:, ps]
+            tab_ref[0:192, base + SB : base + 2 * SB] = steps[:, ps]
+            tab_ref[0:192, base + 2 * SB : base + 3 * SB] = jnp.zeros((192, SB), BF16)
+            tab_ref[192:256, base : base + 2 * SB] = jnp.zeros((64, 2 * SB), BF16)
+            tab_ref[192:256, base + 2 * SB : base + 3 * SB] = la[:, ps]
+        skip_ref[:, n * E : (n + 1) * E] = skip[k : k + 1, :]
 
     for copy in copies:
         copy.wait()
-    left_ref[...] = halo_ref[0]
-    right_ref[...] = halo_ref[1]
+    blocks = tok_ref.shape[0]
+    lane = lax.broadcasted_iota(jnp.int32, (8, SB), 1)
+    row = lax.broadcasted_iota(jnp.int32, (8, SB), 0)
+    rows = [jnp.where(me > 0, halo_ref[0], -1)] + [tok_ref[b] for b in range(blocks)]
+    rows.append(jnp.where(me < count - 1, halo_ref[1], -1))
+    rows = [jnp.broadcast_to(v, (8, SB)) for v in rows]
+    for b in range(blocks):
+        before, here, after = rows[b : b + 3]
+        out = jnp.where(row == KW - 1, here, -1)
+        for shift in range(1, KW):
+            down_by = jnp.where(lane < shift, pltpu.roll(before, shift, 1), pltpu.roll(here, shift, 1))
+            up_by = jnp.where(
+                lane >= SB - shift, pltpu.roll(after, SB - shift, 1), pltpu.roll(here, SB - shift, 1)
+            )
+            out = jnp.where(row == KW - 1 - shift, down_by, out)
+            out = jnp.where(row == KW - 1 + shift, up_by, out)
+        taps_ref[:, b * SB : (b + 1) * SB] = out
 
 
 def compose(earlier, later):
@@ -355,39 +405,27 @@
     count = lax.axis_size("seq")
     blocks = rows // SB
     chunks = rows // CH
-    rim = KW - 1
-
-    hp = jnp.concatenate([jnp.repeat(v, CH, axis=1) for v in (dt_bias, decay_rate, skip_gain)])
-    skip = jnp.concatenate([hp[4 + k] for _, k, _ in CHAINS])[None, :]
-    emb8 = jnp.pad(embed_table, ((0, 3), (0, 0)))
-    wo = jnp.stack([output_weight_matrix, output_weight_matrix[:, ::-1]])
+
     vmem = pl.BlockSpec(memory_space=pltpu.VMEM)
-
-    token_rows = token_ids.reshape(rows // SB, 1, SB)
-    ct, la3, dt3, gate3, score, left, right = pl.pallas_call(
+    token_rows = token_ids.reshape(blocks, 1, SB)
+    tab, la3, gate3, score, skip, taps = pl.pallas_call(
         functools.partial(tables_kernel, count),
         out_shape=(
-            jax.ShapeDtypeStruct((192, 4 * E), BF16),
-            jax.ShapeDtypeStruct((24, 4 * E), BF16),
+            jax.ShapeDtypeStruct((256, 12 * E), BF16),
             jax.ShapeDtypeStruct((24, 4 * E), BF16),
             jax.ShapeDtypeStruct((24, 2 * E), BF16),
             jax.ShapeDtypeStruct((2, 8, 8, SB), F32),
-            jax.ShapeDtypeStruct((1, SB), jnp.int32),
-            jax.ShapeDtypeStruct((1, SB), jnp.int32),
+            jax.ShapeDtypeStruct((1, 4 * E), F32),
+            jax.ShapeDtypeStruct((8, rows), jnp.int32),
         ),
-        in_specs=[vmem] * 5,
-        out_specs=(vmem,) * 7,
+        in_specs=[vmem] * 7,
+        out_specs=(vmem,) * 6,
         scratch_shapes=[
             pltpu.VMEM((2, 1, SB), jnp.int32), pltpu.SemaphoreType.DMA((2,)), pltpu.SemaphoreType.DMA((2,))
         ],
         compiler_params=pltpu.CompilerParams(collective_id=0, has_side_effects=True),
         name="tables",
-    )(token_rows, embed_table, input_weight_matrix, conv_weight, hp)
-    me = lax.axis_index("seq")
-    left = jnp.where(me > 0, left[0, SB - rim :], -1)
-    right = jnp.where(me < count - 1, right[0, :rim], -1)
-    ext = jnp.concatenate([left, token_ids, right])
-    taps = jnp.stack([ext[j : j + rows] for j in range(2 * rim + 1)] + [jnp.full((rows,), -1, jnp.int32)])
+    )(token_rows, embed_table, input_weight_matrix.T, conv_weight, dt_bias, decay_rate, skip_gain)
 
     whole = lambda shape: pl.BlockSpec(shape, lambda i: (0,) * len(shape))
     params = pltpu.CompilerParams(vmem_limit_bytes=56 * 1024 * 1024)
@@ -401,9 +439,7 @@
         ),
         in_specs=[
             pl.BlockSpec((8, SB), lambda i: (0, i)),
-            whole((192, 4 * E)),
-            whole((24, 4 * E)),
-            whole((24, 4 * E)),
+            whole((256, 12 * E)),
             whole((2, 8, 8, SB)),
             whole((1, 4 * E)),
         ],
@@ -415,7 +451,7 @@
         scratch_shapes=[pltpu.VMEM((4, 8, E), F32), pltpu.VMEM((4, 8, E), F32)],
         compiler_params=params,
         name="local_chunks",
-    )(taps, ct, la3, dt3, score, skip)
+    )(taps, tab, score, skip)
 
     nz, ny = NZ, count // (NZ * CORES)
     state = pltpu.VMEM((16, E), F32)
@@ -447,17 +483,17 @@
             whole((2, 8, 8, SB)),
             whole((24, 2 * E)),
             whole((2, E)),
-            whole((8, D)),
-            whole((2, E, D)),
+            whole((5, D)),
+            whole((E, D)),
             whole((chunks, 4, 8, E)),
             whole((2, 16, E)),
             pl.BlockSpec((SB, 4 * E), lambda i: (i, 0)),
         ],
         out_specs=pl.BlockSpec((SB, D), lambda i: (i, 0)),
-        scratch_shapes=[pltpu.VMEM((chunks, 4, 24, E), F32)],
+        scratch_shapes=[pltpu.VMEM((chunks, 4, 24, E), F32), pltpu.VMEM((E, D), BF16)],
         compiler_params=params,
         name="finish_rows",
-    )(taps, la3, score, gate3, norm_gain, emb8, wo, u, far, y)
+    )(taps, la3, score, gate3, norm_gain, embed_table, output_weight_matrix, u, far, y)
 
 
 def solution(mesh):

time: 103 us -> 88.6 us (0.86)
  local copies, waits for them, and re-layouts: 11.8 us -> 0 us
  other arithmetic: 4.73 us -> 0 us
  Pallas kernels: 85.5 us -> 88.4 us
    rev x1 -> x0, local copies, waits for them, and re-layouts: 3.52 us -> none  [per_device(): wo = jnp.stack([output_weight_matrix, output_weight_matrix[:, ::-1]])]
    broadcast_in_dim x7 -> x0, local copies, waits for them, and re-layouts: 2.54 us -> none  [per_device(): jnp.repeat(v, CH, axis=1)]
    concatenate x3 -> x0, other arithmetic: 2.21 us -> none  [the longest x1 0.98 us: per_device(): ext = jnp.concatenate([left, token_ids, right])]
    unnamed x1 -> x0, local copies, waits for them, and re-layouts: 2.12 us -> none
    another operation x1 -> x0, other arithmetic: 1.79 us -> none  [per_device(): wo = jnp.stack([output_weight_matrix, output_weight_matrix[:, ::-1]])]
    pallas_call x1, Pallas kernels: 32.4 us -> 34.1 us  [per_device(): pl.pallas_call(local_kernel, grid=(blocks,), out_shape=(jax.ShapeDtypeStr...]
    another operation x2 -> x0, local copies, waits for them, and re-layouts: 1.34 us -> none  [per_device(): jnp.stack([ext[j:j + rows] for j in range(2 * rim + 1)] + [jnp.full((rows...]
    pad x1 -> x0, local copies, waits for them, and re-layouts: 1.28 us -> none  [per_device(): emb8 = jnp.pad(embed_table, ((0, 3), (0, 0)))]
where the time goes in v3:
time: 88.6 us; the launch traced here: 88.4 us
  Pallas kernels  88.4 us (100%)
    pallas_call x1, Pallas kernels, per_device(): pl.pallas_call(local_kernel, grid=(blocks,), out_shape=(jax.ShapeDtypeStr...  34.1 us
    pallas_call x1, Pallas kernels, per_device(): pl.pallas_call(functools.partial(finish_kernel, chunks), grid=(blocks,),...  21.6 us
    pallas_call x1, Pallas kernels, per_device(): pl.pallas_call(functools.partial(scan_kernel, count), out_shape=jax.Shape...  19.8 us
    pallas_call x1, Pallas kernels, per_device(): pl.pallas_call(functools.partial(tables_kernel, count), out_shape=(jax.Sh...  12.8 us

profile of v3, /device:TPU:1, one launch (start us, length us, event | category | flops | bytes accessed | tf_op | source)
XLA Modules:
  0.0 88.4 jit_solution(15468355277172548670)
XLA Ops:
  0.0 12.8 %tables.1 = (bf16[256,6144]{1,0:T(8,128)(2,1)}, bf16[24,2048]{1,0:T(8,128)(2,1)}, bf16[24,1024]{1,0:T(8,128)(2,1)}, f32[2,8,8,128]{3,2,1,0:T(8,128)}, f32[1,2048]{1,0:T(1,128)}, /*index=5*/s32[8,1024]{1,0:T(8,128)}) custom-call(s32[8,1,128]{2,1,0:T(1,128)} %bitcast.5, bf16[5,256]{1,0:T(8,128)(2,1)} %emb_ref.3, bf16[1064,256]{1,0:T(8,128)(2,1)} %bitcast.3, ...), custom_call_target="tpu_custom_call" | custom-call | tf_op jit(solution)/shard_map/tables/pallas_call | solution.py:411
  12.8 34.1 %local_chunks.1 = (f32[1024,2048]{1,0:T(8,128)}, f32[16,4,8,512]{3,2,1,0:T(8,128)}, f32[4,8,512]{2,1,0:T(8,128)}) custom-call(s32[8,1024]{1,0:T(8,128)} %get-tuple-element.14.taps_ref, bf16[256,6144]{1,0:T(8,128)(2,1)} %get-tuple-element.18.tab_ref, f32[2,8,8,128]{3,2,1,0:T(8,128)} %get-tuple-element.16.s_ref, f32[1,2048]{1,0:T(1,128)} %get-tuple-element.19.skip_ref), custom_call_target="tpu_custom_call" | custom-call | tf_op jit(solution)/shard_map/local_chunks/pallas_call | solution.py:432
  47.0 19.8 %state_scan.1.far_ref = f32[2,16,512]{2,1,0:T(8,128)} custom-call(f32[2,16,512]{2,1,0:T(8,128)} %bitcast.4), custom_call_target="tpu_custom_call" | custom-call | tf_op jit(solution)/shard_map/state_scan/pallas_call | solution.py:458
  66.8 21.6 %finish_rows.1 = bf16[1024,256]{1,0:T(8,128)(2,1)} custom-call(s32[8,1024]{1,0:T(8,128)} %get-tuple-element.14.taps_ref, bf16[24,2048]{1,0:T(8,128)(2,1)} %get-tuple-element.15.la_ref, f32[2,8,8,128]{3,2,1,0:T(8,128)} %get-tuple-element.16.s_ref, bf16[24,1024]{1,0:T(8,128)(2,1)} %get-tuple-element.17.gate_ref, f32[2,512]{1,0:T(2,128)} %gain_ref.3, ...), custom_call_target="tpu_custom_call" | custom-call | tf_op jit(solution)/shard_map/finish_rows/pallas_call | solution.py:476

commit v4 on v3

--- a/solution.py
+++ b/solution.py
@@ -17,6 +17,7 @@
 EPSILON = 1e-05
 LOG2E = 1.4426950408889634
 CORES = 2
+WIDE = 4
 NZ = 8
 CHAINS = ((0, 0, False), (1, 1, False), (0, 1, True), (1, 0, True))
 MESH = pl.DeviceIdType.MESH
@@ -61,11 +62,19 @@
         dacc_ref[...] = jnp.zeros_like(dacc_ref)
         eacc_ref[...] = jnp.zeros_like(eacc_ref)
 
-    oht = onehots(taps_ref[...])
-    oh = jnp.concatenate(oht, axis=0).T.astype(BF16)
-    center = jnp.concatenate([oht[3]] * 3 + [jnp.zeros_like(oht[3])] * 5, axis=0).T.astype(BF16)
-    keys = [jnp.concatenate([oh, oh, oh, counts(center, backward)], axis=1) for backward in (False, True)]
-    center = center[:, :24]
+    centers, keys, ot2 = [], [[], []], []
+    lane8 = lax.broadcasted_iota(jnp.int32, (8, SB), 1)
+    row8 = lax.broadcasted_iota(jnp.int32, (8, SB), 0)
+    for part in range(WIDE):
+        oht = onehots(taps_ref[:, part * SB : (part + 1) * SB])
+        oh = jnp.concatenate(oht, axis=0).T.astype(BF16)
+        center = jnp.concatenate([oht[3]] * 3 + [jnp.zeros_like(oht[3])] * 5, axis=0).T.astype(BF16)
+        for d in range(2):
+            keys[d].append(jnp.concatenate([oh, oh, oh, counts(center, d == 1)], axis=1))
+        centers += [center[:CH, :24], center[CH:, :24]]
+        rolled = pltpu.roll(oht[3], CH, 1)
+        ot2 += [jnp.where(lane8 < CH, oht[3], rolled), jnp.where(lane8 < CH, rolled, oht[3])]
+    keys = [jnp.concatenate(v, axis=0) for v in keys]
 
     lane = lax.broadcasted_iota(jnp.int32, (CH, SB), 1)
     row = lax.broadcasted_iota(jnp.int32, (CH, SB), 0)
@@ -76,20 +85,15 @@
         jnp.where(within <= row, 0.0, -1e30).astype(F32),
         jnp.where(within >= row, 0.0, -1e30).astype(F32),
     )
-    lane8 = lax.broadcasted_iota(jnp.int32, (8, SB), 1)
-    row8 = lax.broadcasted_iota(jnp.int32, (8, SB), 0)
-    rolled = pltpu.roll(oht[3], CH, 1)
-    ot2 = (jnp.where(lane8 < CH, oht[3], rolled), jnp.where(lane8 < CH, rolled, oht[3]))
-
     scores = []
     for strand in range(2):
         per_chunk = []
-        for c in range(2):
+        for c in range(2 * WIDE):
             acc = None
             for b in range(5):
                 term = s_ref[strand, b] * ot2[c][b : b + 1, :]
                 acc = term if acc is None else acc + term
-            per_chunk.append(dot(center[c * CH : (c + 1) * CH], stack3(acc)))
+            per_chunk.append(dot(centers[c], stack3(acc)))
         scores.append(per_chunk)
 
     for n, (strand, k, backward) in enumerate(CHAINS):
@@ -104,7 +108,7 @@
             cum = found[:, 2 * SB :]
             xh = xw.astype(BF16)
             xl = (xw - xh.astype(F32)).astype(BF16)
-            for c in range(2):
+            for c in range(2 * WIDE):
                 rows = slice(c * CH, (c + 1) * CH)
                 cc = cum[rows]
                 rowv = jnp.sum(jnp.where(diag, cc, 0.0), axis=0, keepdims=True)
@@ -148,10 +152,12 @@
         r = lax.broadcasted_iota(jnp.int32, (D, D), 0)
         c = lax.broadcasted_iota(jnp.int32, (D, D), 1)
         rev_ref[...] = dot(wo_ref[...], (r + c == D - 1).astype(BF16)).astype(BF16)
-        for n, (strand, k, backward) in enumerate(CHAINS):
-
-            def chunk(i, s):
+
+        def chunk(i, states):
+            following = []
+            for n, (strand, k, backward) in enumerate(CHAINS):
                 c = chunks - 1 - i if backward else i
+                s = states[n]
                 acc = None
                 for b in range(5):
                     col = s_ref[strand, b]
@@ -162,9 +168,11 @@
                     [hi.astype(F32), mid.astype(F32), lo.astype(F32)], axis=0
                 )
                 piece = u_ref[c, n]
-                return jnp.exp2(piece[5:6, :]) * s + piece
-
-            lax.fori_loop(0, chunks, chunk, far_ref[int(backward), (n % 2) * 8 : (n % 2) * 8 + 8, :])
+                following.append(jnp.exp2(piece[5:6, :]) * s + piece)
+            return tuple(following)
+
+        start = tuple(far_ref[n // 2, (n % 2) * 8 : (n % 2) * 8 + 8, :] for n in range(4))
+        lax.fori_loop(0, chunks, chunk, start, unroll=2)
 
     center = (
         taps_ref[3:4, :] == lax.broadcasted_iota(jnp.int32, (SB, SB), 0) % 8
@@ -174,6 +182,9 @@
     c = lax.broadcasted_iota(jnp.int32, (2 * SB, SB), 1)
     ones = (((r % SB) // CH) == (c // CH)).astype(BF16)
 
+    upper = lax.broadcasted_iota(jnp.int32, (SB, 24), 0) < CH
+    wide = center.astype(F32)
+    placed = jnp.concatenate([jnp.where(upper, wide, 0.0), jnp.where(upper, 0.0, wide)], axis=1).astype(BF16)
     total = dot(center[:, :5], emb_ref[...])
     for strand in range(2):
         mixed = []
@@ -186,24 +197,23 @@
                 backward = CHAINS[n][2]
                 cols = slice(n * E + half * 2 * SB, n * E + (half + 1) * 2 * SB)
                 reach = jnp.exp2(dot(cnt[int(backward)], la_ref[:, cols]))
-                far = jnp.concatenate(
-                    [
-                        dot(center[h * CH : (h + 1) * CH], in_ref[step * 2 + h, n, :, ps].astype(BF16))
-                        for h in range(2)
-                    ],
-                    axis=0,
-                )
+                entry = jnp.concatenate([in_ref[step * 2, n, :, ps], in_ref[step * 2 + 1, n, :, ps]], axis=0)
+                far = dot(placed, entry.astype(BF16))
                 g = (y_ref[:, cols] + reach * far) * gate
                 sq = g * g
                 sh = sq.astype(BF16)
                 sl = (sq - sh.astype(F32)).astype(BF16)
-                mean = jnp.concatenate(
-                    [
-                        dot(jnp.concatenate([sh[:, q * SB : (q + 1) * SB], sl[:, q * SB : (q + 1) * SB]], axis=1), ones)
-                        for q in range(2)
-                    ],
-                    axis=1,
-                ) * (1.0 / CH)
+                mean = dot(
+                    jnp.concatenate(
+                        [
+                            jnp.concatenate([v[:, q * SB : (q + 1) * SB] for v in (sh, sl)], axis=1)
+                            for q in range(2)
+                        ],
+                        axis=0,
+                    ),
+                    ones,
+                )
+                mean = jnp.concatenate([mean[:SB], mean[SB:]], axis=1) * (1.0 / CH)
                 normed = g * lax.rsqrt(mean + EPSILON) * gain_ref[k : k + 1, ps]
                 acc = normed if acc is None else acc + normed
             mixed.append(acc.astype(BF16))
@@ -431,21 +441,21 @@
     params = pltpu.CompilerParams(vmem_limit_bytes=56 * 1024 * 1024)
     y, u, end = pl.pallas_call(
         local_kernel,
-        grid=(blocks,),
+        grid=(blocks // WIDE,),
         out_shape=(
             jax.ShapeDtypeStruct((rows, 4 * E), F32),
             jax.ShapeDtypeStruct((chunks, 4, 8, E), F32),
             jax.ShapeDtypeStruct((4, 8, E), F32),
         ),
         in_specs=[
-            pl.BlockSpec((8, SB), lambda i: (0, i)),
+            pl.BlockSpec((8, WIDE * SB), lambda i: (0, i)),
             whole((256, 12 * E)),
             whole((2, 8, 8, SB)),
             whole((1, 4 * E)),
         ],
         out_specs=(
-            pl.BlockSpec((SB, 4 * E), lambda i: (i, 0)),
-            pl.BlockSpec((2, 4, 8, E), lambda i: (i, 0, 0, 0)),
+            pl.BlockSpec((WIDE * SB, 4 * E), lambda i: (i, 0)),
+            pl.BlockSpec((2 * WIDE, 4, 8, E), lambda i: (i, 0, 0, 0)),
             whole((4, 8, E)),
         ),
         scratch_shapes=[pltpu.VMEM((4, 8, E), F32), pltpu.VMEM((4, 8, E), F32)],

time: 88.6 us -> 66.6 us (0.75)
  Pallas kernels: 88.4 us -> 66.3 us
    pallas_call x1, Pallas kernels: 34.1 us -> 16 us  [per_device(): pl.pallas_call(local_kernel, grid=(blocks // WIDE,), out_shape=(jax.Shape...]
    pallas_call x1, Pallas kernels: 21.6 us -> 17.6 us  [per_device(): pl.pallas_call(functools.partial(finish_kernel, chunks), grid=(blocks,),...]
where the time goes in v4:
time: 66.6 us; the launch traced here: 66.3 us
  Pallas kernels  66.3 us (100%)
    pallas_call x1, Pallas kernels, per_device(): pl.pallas_call(functools.partial(scan_kernel, count), out_shape=jax.Shape...  19.9 us
    pallas_call x1, Pallas kernels, per_device(): pl.pallas_call(functools.partial(finish_kernel, chunks), grid=(blocks,),...  17.6 us
    pallas_call x1, Pallas kernels, per_device(): pl.pallas_call(local_kernel, grid=(blocks // WIDE,), out_shape=(jax.Shape...  16 us
    pallas_call x1, Pallas kernels, per_device(): pl.pallas_call(functools.partial(tables_kernel, count), out_shape=(jax.Sh...  12.8 us

profile of v4, /device:TPU:1, one launch (start us, length us, event | category | flops | bytes accessed | tf_op | source)
XLA Modules:
  0.0 66.3 jit_solution(8536852871418336731)
XLA Ops:
  0.0 12.8 %tables.1 = (bf16[256,6144]{1,0:T(8,128)(2,1)}, bf16[24,2048]{1,0:T(8,128)(2,1)}, bf16[24,1024]{1,0:T(8,128)(2,1)}, f32[2,8,8,128]{3,2,1,0:T(8,128)}, f32[1,2048]{1,0:T(1,128)}, /*index=5*/s32[8,1024]{1,0:T(8,128)}) custom-call(s32[8,1,128]{2,1,0:T(1,128)} %bitcast.5, bf16[5,256]{1,0:T(8,128)(2,1)} %emb_ref.3, bf16[1064,256]{1,0:T(8,128)(2,1)} %bitcast.3, ...), custom_call_target="tpu_custom_call" | custom-call | tf_op jit(solution)/shard_map/tables/pallas_call | solution.py:421
  12.8 16.0 %local_chunks.1 = (f32[1024,2048]{1,0:T(8,128)}, f32[16,4,8,512]{3,2,1,0:T(8,128)}, f32[4,8,512]{2,1,0:T(8,128)}) custom-call(s32[8,1024]{1,0:T(8,128)} %get-tuple-element.14.taps_ref, bf16[256,6144]{1,0:T(8,128)(2,1)} %get-tuple-element.18.tab_ref, f32[2,8,8,128]{3,2,1,0:T(8,128)} %get-tuple-element.16.s_ref, f32[1,2048]{1,0:T(1,128)} %get-tuple-element.19.skip_ref), custom_call_target="tpu_custom_call" | custom-call | tf_op jit(solution)/shard_map/local_chunks/pallas_call | solution.py:442
  28.8 19.9 %state_scan.1.far_ref = f32[2,16,512]{2,1,0:T(8,128)} custom-call(f32[2,16,512]{2,1,0:T(8,128)} %bitcast.4), custom_call_target="tpu_custom_call" | custom-call | tf_op jit(solution)/shard_map/state_scan/pallas_call | solution.py:468
  48.7 17.6 %finish_rows.1 = bf16[1024,256]{1,0:T(8,128)(2,1)} custom-call(s32[8,1024]{1,0:T(8,128)} %get-tuple-element.14.taps_ref, bf16[24,2048]{1,0:T(8,128)(2,1)} %get-tuple-element.15.la_ref, f32[2,8,8,128]{3,2,1,0:T(8,128)} %get-tuple-element.16.s_ref, bf16[24,1024]{1,0:T(8,128)(2,1)} %get-tuple-element.17.gate_ref, f32[2,512]{1,0:T(2,128)} %gain_ref.3, ...), custom_call_target="tpu_custom_call" | custom-call | tf_op jit(solution)/shard_map/finish_rows/pallas_call | solution.py:486
